TPU v7x, 512 devices: a whole 4x4x16 slice. The times are simulated.
512 devices in a mesh: view: 8 (over y, x_lo), batch: 64 (over x_hi, z, core).
Axes of the slice: x: 4 (x_hi: 2, x_lo: 2; x = x_hi * 2 + x_lo), y: 4, z: 16, core: 2. Of those that a mesh axis runs over, the one named last changes fastest.
Arguments:
- embeddings: bfloat16 [8, 8192, 256], P('view', 'batch'), may hold values from -1.5 to 1.5
- positive: int32 [8, 8192], P(None, 'batch'), may hold values from 0 to 127, as said below
Outputs:
- gradients: float32 [8, 8192, 256], P('view', 'batch')
- totals: float32 [8, 8192], P('view', 'batch')
- row_loss: float32 [8, 8192], P('view', 'batch')
Inputs may be any that keep to these rules, and one draw needn't show every extreme that they name: `positive`: for each view and each aligned block of 128 samples, the entries are a permutation of 0 to 127.
All inputs are finite; a program needn't handle non-finite values.
Results may differ from a plain program's by a relative error of at most 0.002.
Values may be sent and summed in bfloat16 or wider, within the bound.
No kernel may reach another device: no remote copies, remote signals or barrier semaphores. Data moves between devices by JAX's collectives and lax.ppermute only.
A program may use at most 64 MiB of HBM per device.

v0:
```python
import jax
import jax.numpy as jnp
from jax import lax
from jax.sharding import PartitionSpec as P

logit_scale = 10.0


def from_partner(value, axis, bit):
    return lax.ppermute(value, axis, [(i, i ^ 1 << bit) for i in range(lax.axis_size(axis))])


def body(embeddings, positive):
    own_rows = embeddings[0]
    row_count = own_rows.shape[0]
    view_count = lax.axis_size("view")
    swap_bit = view_count.bit_length() - 2
    partner = from_partner(own_rows, "view", swap_bit)
    view_index = lax.axis_index("view")
    own_match = lax.dynamic_index_in_dim(positive, view_index, 0, keepdims=False)
    far_match = lax.dynamic_index_in_dim(
        positive, jnp.bitwise_xor(view_index, view_count // 2), 0, keepdims=False
    )

    def score_piece(key_piece):
        return (
            jnp.einsum("ie,je->ij", own_rows, key_piece, preferred_element_type=jnp.float32)
            * logit_scale
        )

    running_max = jnp.full((row_count,), -1e30, jnp.float32)
    scores = score_piece(lax.all_gather(partner, "batch", axis=0, tiled=True))
    new_max = jnp.maximum(running_max, jnp.max(scores, axis=1))
    summed = jnp.sum(jnp.exp(scores - new_max[:, None]), axis=1)
    running_max, summed = (new_max, summed)
    totals = running_max + jnp.log(summed)
    far_totals = from_partner(totals, "view", swap_bit)
    every_total = lax.all_gather(far_totals, "batch", axis=0, tiled=True)
    key_piece = lax.all_gather(partner, "batch", axis=0, tiled=True)
    scores = score_piece(key_piece)
    w_rows = jnp.exp(scores - totals[:, None]).astype(jnp.bfloat16)
    w_cols = jnp.exp(scores - every_total[None, :]).astype(jnp.bfloat16)
    products = jnp.dot(
        jnp.concatenate([w_rows, w_cols], axis=0), key_piece, preferred_element_type=jnp.float32
    )
    own_acc = products[:row_count]
    side_acc = products[row_count:]
    spread = own_acc + side_acc
    pos_rows = jnp.take(partner, own_match, axis=0).astype(jnp.float32)
    pos_score = jnp.sum(own_rows.astype(jnp.float32) * pos_rows, axis=1) * logit_scale
    row_loss = totals - pos_score
    row_ids = jnp.arange(row_count, dtype=jnp.int32)
    matched_hot = (far_match[None, :] == row_ids[:, None]).astype(jnp.bfloat16)
    matched = jnp.dot(matched_hot, partner, preferred_element_type=jnp.float32)
    gradients = logit_scale * (spread - pos_rows - matched)
    return (gradients[None], totals[None], row_loss[None])


def solution(mesh):
    return jax.shard_map(
        body,
        mesh=mesh,
        in_specs=(P("view", "batch", None), P(None, "batch")),
        out_specs=(P("view", "batch", None), P("view", "batch"), P("view", "batch")),
        check_vma=False,
    )
```

profile of v0, /device:TPU:1, one launch (start us, length us, event | category | flops | bytes accessed | tf_op | source)
XLA Modules:
  0.0 268.4 jit_solution(11104582229734057468)
XLA Ops:
  7.2 0.0 all-gather.3.cloned.1.call-start
  7.2 5.6 %collective-permute-start = (bf16[128,256]{1,0:T(8,128)(2,1)}, bf16[128,256]{1,0:T(8,128)(2,1)S(1)}, u32[]{:S(2)}, u32[]{:S(2)}) collective-permute-start(bf16[128,256]{1,0:T(8,128)(2,1)} %bitcast.25), channel_id=1, source_target_pairs={{0,256},{64,320},{128,384},{192,448},{256,0},{320,64},{384,128},{4... | collective-permute-start | bytes 196616 | tf_op jit(solution)/shard_map/ppermute | solution.py:10
  12.9 1.9 collective-permute-done
  14.7 0.0 copy-start
  14.7 0.6 copy-done
  15.3 0.0 all-gather.3.cloned.1.call-update
  15.4 0.7 fusion.10
  16.1 0.7 compare_and_fusion
  16.8 0.7 dynamic-slice_bitcast_fusion
  17.5 1.6 gather_fusion
  19.1 1.0 fusion.7
  20.1 152.4 %all-gather.3.cloned.1.call-done = bf16[8192,256]{1,0:T(8,128)(2,1)} async-done(((bf16[128,256]{1,0:T(8,128)(2,1)}), bf16[8192,256]{1,0:T(8,128)(2,1)}) %all-gather.3.cloned.1.call-update) | async-done | bytes 4194320 | tf_op jit(solution)/shard_map/all_gather | solution.py:39
  172.5 3.8 %fusion.13 = (f32[128]{0:T(128)S(1)}, f32[128,8192]{1,0:T(8,128)S(1)}) fusion(bf16[8192,256]{1,0:T(8,128)(2,1)} %all-gather.3.cloned.1.call-done, bf16[1,128,256]{2,1,0:T(8,128)(2,1)} %param.2), kind=kOutput, calls=%fused_computation.32 | convolution fusion | flops 538967936 | bytes 8454656 | tf_op jit(solution)/shard_map/ie,je->ij/dot_general | solution.py:27
  176.3 0.8 exponential_reduce_fusion
  177.0 0.0 copy-start.3
  177.1 4.6 %collective-permute-start.1 = (f32[128]{0:T(128)S(1)}, f32[128]{0:T(128)S(1)}, u32[]{:S(2)}, u32[]{:S(2)}) collective-permute-start(f32[128]{0:T(128)S(1)} %log_add_fusion), channel_id=1, source_target_pairs={{0,256},{64,320},{128,384},{192,448},{256,0},{320,64},{384,128},{4... | collective-permute-start | bytes 1544 | tf_op jit(solution)/shard_map/ppermute | solution.py:10
  181.7 0.5 bitcast_subtract_fusion
  182.2 0.7 collective-permute-done.1
  182.9 74.4 %all-gather = f32[64,1,128]{2,1,0:T(1,128)S(1)} all-gather(f32[1,1,128]{2,1,0:T(1,128)S(1)} %bitcast.28), channel_id=1, replica_groups=mesh['view'=8,'batch'=64] {'batch'}, dimensions={0}, use_global_device_ids=true | all-gather | bytes 33280 | tf_op jit(solution)/shard_map/all_gather | solution.py:38
  257.3 0.0 copy-start.2
  257.3 1.5 exponential_convert_fusion.1
  258.7 0.0 copy-done.3
  258.8 0.7 copy-done.2
  259.5 0.0 copy-start.1
  259.5 1.2 fusion
  260.7 0.0 copy-done.1
  260.7 0.8 fusion.6
  (3 shorter events, 0.0 us)
Async XLA Ops:
  7.2 165.3 %all-gather.3.cloned.1.call-start = ((), (), s32[]{:S(2)}) async-start(), calls=%async_computation | async-start | bytes 4259840 | tf_op jit(solution)/shard_map/all_gather | solution.py:39
  7.2 7.5 %collective-permute-start = (bf16[128,256]{1,0:T(8,128)(2,1)}, bf16[128,256]{1,0:T(8,128)(2,1)S(1)}, u32[]{:S(2)}, u32[]{:S(2)}) collective-permute-start(bf16[128,256]{1,0:T(8,128)(2,1)} %bitcast.25), channel_id=1, source_target_pairs={{0,256},{64,320},{128,384},{192,448},{256,0},{320,64},{384,128},{4... | collective-permute-start | bytes 196616 | tf_op jit(solution)/shard_map/ppermute | solution.py:10
  14.7 0.6 copy-start
  177.0 81.7 %copy-start.3 = (f32[128]{0:T(128)}, f32[128]{0:T(128)S(1)}, u32[]{:S(2)}) copy-start(f32[128]{0:T(128)S(1)} %log_add_fusion) | copy-start | bytes 1540
  177.1 5.8 %collective-permute-start.1 = (f32[128]{0:T(128)S(1)}, f32[128]{0:T(128)S(1)}, u32[]{:S(2)}, u32[]{:S(2)}) collective-permute-start(f32[128]{0:T(128)S(1)} %log_add_fusion), channel_id=1, source_target_pairs={{0,256},{64,320},{128,384},{192,448},{256,0},{320,64},{384,128},{4... | collective-permute-start | bytes 1544 | tf_op jit(solution)/shard_map/ppermute | solution.py:10
  257.3 2.2 copy-start.2
  259.5 1.3 copy-start.1
Sparse Core Ops, SparseCore 0:
  15.5 156.9 all-gather.2
where the time goes:
time: 269 us; the launch traced here: 268 us
  waiting for transfers between devices  155 us (58%)
  blocking collectives  74.4 us (28%)
  between operations  14.1 us (5%)
  starting transfers between devices  10.3 us (4%)
  matrix products  5.86 us (2%)
  other arithmetic  5.15 us (2%)
  local copies, waits for them, and re-layouts  3.66 us (1%)
    all_gather x1, waiting for transfers between devices, body(): key_piece = lax.all_gather(partner, 'batch', axis=0, tiled=True)  152 us
    all_gather x1, blocking collectives, body(): every_total = lax.all_gather(far_totals, 'batch', axis=0, tiled=True)  74.4 us
    ppermute x2, starting transfers between devices, from_partner(): lax.ppermute(value, axis, [(i, i ^ 1 << bit) for i in range(lax.axis_size...  10.3 us
  transfers between devices with their start and end apart: 3, of which 3 were waited for; matrix products, arithmetic and copies ran while one was open for 2% of the time, Pallas kernels for 0%

commit v1 on v0

v1 whole, which is shorter than its diff:
```python
import jax
import jax.numpy as jnp
from jax import lax
from jax.experimental import pallas as pl
from jax.experimental.pallas import tpu as pltpu
from jax.sharding import Mesh, PartitionSpec as P

logit_scale = 10.0

PAIR, REST = "pair", "rest"
XH, ZP, Z0, CORE = "xh", "zp", "z0", "core"
ROW_GROUP = (XH, Z0, CORE)
COL_GROUP = (ZP,)
VMEM = pl.BlockSpec(memory_space=pltpu.VMEM)


def score_block(rows, cols):
    return (
        lax.dot_general(rows, cols, (((1,), (1,)), ((), ())), preferred_element_type=jnp.float32)
        * logit_scale
    )


def combine(parts):
    top = jnp.max(parts, axis=0)
    return top + jnp.log(jnp.sum(jnp.exp(parts - top[None]), axis=0))


def lse_kernel(row_ref, col_ref, row_lse_ref, col_lse_ref, score_ref):
    step = 256
    for left, right, out in ((row_ref, col_ref, col_lse_ref), (col_ref, row_ref, row_lse_ref)):
        count, width = left.shape[0], right.shape[0]
        top = jnp.full((8, width), -1e30, jnp.float32)
        for start in range(0, count, step):
            block = score_block(left[start : start + step, :], right[...])
            score_ref[start : start + step, :] = block
            top = jnp.maximum(top, jnp.max(block.reshape(step // 8, 8, width), axis=0))
        top = jnp.max(top, axis=0, keepdims=True)
        total = jnp.zeros((8, width), jnp.float32)
        for start in range(0, count, step):
            block = jnp.exp(score_ref[start : start + step, :] - top)
            total = total + jnp.sum(block.reshape(step // 8, 8, width), axis=0)
        lse = top + jnp.log(jnp.sum(total, axis=0, keepdims=True))
        tile = jnp.concatenate([lse[:, i : i + 128] for i in range(0, width, 128)], axis=0)
        for peer in range(out.shape[0]):
            out[peer] = tile


def own_kernel(
    row_ref, col_ref, parts_ref, own_ref, partner_ref, positive_ref,
    grad_ref, totals_ref, loss_ref, base_ref, totals_scratch,
):
    totals = combine(parts_ref[...])
    totals_scratch[...] = totals
    block_rows = totals.shape[1]
    width = col_ref.shape[0]
    for i in range(totals.shape[0]):
        shift = jnp.broadcast_to(totals[i : i + 1, :], (128, block_rows)).T
        scores = score_block(row_ref[i * block_rows : (i + 1) * block_rows, :], col_ref[...])
        weights = jnp.exp(scores - jnp.concatenate([shift] * (width // 128), axis=1))
        grad_ref[i] = jnp.dot(
            weights.astype(jnp.bfloat16), col_ref[...], preferred_element_type=jnp.float32
        )
    rest_count = lax.axis_size(REST)
    pair = lax.axis_index(PAIR)
    view = pair * rest_count + lax.axis_index(REST)
    far = (1 - pair) * rest_count + lax.axis_index(REST)
    own_match = positive_ref[pl.ds(view, 1), :]
    far_match = positive_ref[pl.ds(far, 1), :]
    row_ids = lax.broadcasted_iota(jnp.int32, (block_rows, block_rows), 0)
    own_hot = (row_ids == own_match).astype(jnp.float32).astype(jnp.bfloat16)
    far_hot = (row_ids == far_match).astype(jnp.float32).astype(jnp.bfloat16)
    partner = partner_ref[...]
    pos_rows = lax.dot_general(
        own_hot, partner, (((0,), (0,)), ((), ())), preferred_element_type=jnp.float32
    )
    matched = jnp.dot(far_hot, partner, preferred_element_type=jnp.float32)
    base_ref[...] = (pos_rows + matched) * -logit_scale
    product = own_ref[...].astype(jnp.float32) * pos_rows
    pos_score = jnp.sum(product.T, axis=0, keepdims=True) * logit_scale
    place = (lax.axis_index(XH) * lax.axis_size(Z0) + lax.axis_index(Z0)) * lax.axis_size(CORE)
    place = place + lax.axis_index(CORE)
    own_totals = totals_scratch[pl.ds(place, 1), :]
    totals_ref[...] = own_totals
    loss_ref[...] = own_totals - pos_score


def side_kernel(row_ref, col_ref, parts_ref, own_grad_ref, grad_ref):
    totals = combine(parts_ref[...])
    shift = jnp.concatenate([totals[i : i + 1, :] for i in range(totals.shape[0])], axis=1)
    block_rows = grad_ref.shape[1]
    for i in range(grad_ref.shape[0]):
        scores = score_block(row_ref[i * block_rows : (i + 1) * block_rows, :], col_ref[...])
        weights = jnp.exp(scores - shift)
        grad_ref[i] = own_grad_ref[i] + jnp.dot(
            weights.astype(jnp.bfloat16), col_ref[...], preferred_element_type=jnp.float32
        )


def sum_kernel(parts_ref, base_ref, out_ref):
    total = parts_ref[0]
    for i in range(1, parts_ref.shape[0]):
        total = total + parts_ref[i]
    out_ref[...] = total * logit_scale + base_ref[...]


def call(kernel, outs, *args, flops=0, transcendentals=0, scratch=()):
    single = not isinstance(outs, tuple)
    out_list = (outs,) if single else outs
    moved = sum(a.size * a.dtype.itemsize for a in args)
    moved += sum(o.size * o.dtype.itemsize for o in out_list)
    return pl.pallas_call(
        kernel,
        out_shape=outs,
        in_specs=[VMEM] * len(args),
        out_specs=VMEM if single else tuple([VMEM] * len(out_list)),
        scratch_shapes=list(scratch),
        cost_estimate=pl.CostEstimate(
            flops=flops, bytes_accessed=moved, transcendentals=transcendentals
        ),
    )(*args)


def exchange(value, axes):
    return lax.all_to_all(value, axes, 0, 0, tiled=True)


def body(embeddings, positive):
    own = embeddings[0]
    row_count, width = own.shape
    rows_n = lax.axis_size(XH) * lax.axis_size(Z0) * lax.axis_size(CORE)
    cols_n = lax.axis_size(ZP)
    f32 = jnp.float32
    partner = lax.ppermute(own, PAIR, [(0, 1), (1, 0)])
    rows = exchange(jnp.broadcast_to(own[None], (rows_n, row_count, width)), ROW_GROUP)
    rows = rows.reshape(rows_n * row_count, width)
    cols = lax.all_gather(partner, COL_GROUP, axis=0, tiled=True)
    rows_total, cols_total = rows.shape[0], cols.shape[0]
    area = rows_total * cols_total
    row_parts, col_parts = call(
        lse_kernel,
        (
            jax.ShapeDtypeStruct((rows_n, rows_total // 128, 128), f32),
            jax.ShapeDtypeStruct((cols_n, cols_total // 128, 128), f32),
        ),
        rows, cols,
        flops=4 * area * width, transcendentals=2 * area,
        scratch=[pltpu.VMEM((max(rows_total, cols_total),) * 2, f32)],
    )
    row_parts = exchange(row_parts, ROW_GROUP)
    col_parts = exchange(col_parts, COL_GROUP)
    grads, totals, row_loss, base = call(
        own_kernel,
        (
            jax.ShapeDtypeStruct((rows_n, row_count, width), f32),
            jax.ShapeDtypeStruct((1, row_count), f32),
            jax.ShapeDtypeStruct((1, row_count), f32),
            jax.ShapeDtypeStruct((row_count, width), f32),
        ),
        rows, cols, row_parts, own, partner, positive,
        flops=4 * area * width, transcendentals=area,
        scratch=[pltpu.VMEM((rows_total // 128, 128), f32)],
    )
    grads = call(
        side_kernel,
        jax.ShapeDtypeStruct((rows_n, row_count, width), f32),
        rows, cols, col_parts, grads,
        flops=4 * area * width, transcendentals=area,
    )
    grads = exchange(grads, ROW_GROUP)
    gradients = call(sum_kernel, jax.ShapeDtypeStruct((row_count, width), f32), grads, base)
    return (gradients[None], totals, row_loss)


def solution(mesh):
    view, batch = mesh.shape["view"], mesh.shape["batch"]
    inner = Mesh(
        mesh.devices.reshape(2, view // 2, 2, batch // 8, 2, 2), (PAIR, REST, XH, ZP, Z0, CORE)
    )
    v, b = (PAIR, REST), (XH, ZP, Z0, CORE)
    return jax.shard_map(
        body,
        mesh=inner,
        in_specs=(P(v, b, None), P(None, b)),
        out_specs=(P(v, b, None), P(v, b), P(v, b)),
        check_vma=False,
    )
```

time: 269 us -> 122 us (0.45)
  waiting for transfers between devices: 155 us -> 12.2 us
  Pallas kernels: 0 us -> 15.8 us
  between operations: 14.1 us -> 0.66 us
  starting transfers between devices: 10.3 us -> 19.7 us
  matrix products: 5.86 us -> 0 us
  other arithmetic: 5.15 us -> 0 us
  blocking collectives: 74.4 us -> 69.5 us
    all_gather x1 -> x0, waiting for transfers between devices: 152 us -> none  [body(): key_piece = lax.all_gather(partner, 'batch', axis=0, tiled=True)]
    all_gather x1, blocking collectives: 74.4 us -> 28.9 us  [body(): cols = lax.all_gather(partner, COL_GROUP, axis=0, tiled=True)]
    all_to_all x0 -> x2, blocking collectives: none -> 40.6 us  [exchange(): return lax.all_to_all(value, axes, 0, 0, tiled=True)]
    all_to_all x0 -> x2, starting transfers between devices: none -> 17.8 us  [exchange(): return lax.all_to_all(value, axes, 0, 0, tiled=True)]
    pallas_call x0 -> x4, Pallas kernels: none -> 15.8 us  [call(): pl.pallas_call(kernel, out_shape=outs, in_specs=[VMEM] * len(args), out_s...]
    ppermute x2 -> x1, starting transfers between devices: 10.3 us -> 1.91 us  [body(): partner = lax.ppermute(own, PAIR, [(0, 1), (1, 0)])]
    all_to_all x0 -> x2, waiting for transfers between devices: none -> 7.24 us  [exchange(): return lax.all_to_all(value, axes, 0, 0, tiled=True)]
    dot_general x3 -> x0, matrix products: 5.86 us -> none  [the longest x1 3.8 us: score_piece(): jnp.einsum('ie,je->ij', own_rows, key_piece, preferred_element_type=jnp.f...]
  transfers between devices with their start and end apart: 3 -> 3, of which waited for: 3 -> 2; matrix products, arithmetic and copies ran while one was open for 2% -> 0% of each run, Pallas kernels for 0% -> 4%
where the time goes in v1:
time: 122 us; the launch traced here: 121 us
  blocking collectives  69.5 us (57%)
  starting transfers between devices  19.7 us (16%)
  Pallas kernels  15.8 us (13%)
  waiting for transfers between devices  12.2 us (10%)
  local copies, waits for them, and re-layouts  3.08 us (3%)
    all_to_all x2, blocking collectives, exchange(): return lax.all_to_all(value, axes, 0, 0, tiled=True)  40.6 us
    all_gather x1, blocking collectives, body(): cols = lax.all_gather(partner, COL_GROUP, axis=0, tiled=True)  28.9 us
    all_to_all x2, starting transfers between devices, exchange(): return lax.all_to_all(value, axes, 0, 0, tiled=True)  17.8 us
    pallas_call x4, Pallas kernels, call(): pl.pallas_call(kernel, out_shape=outs, in_specs=[VMEM] * len(args), out_s...  15.8 us
    all_to_all x2, waiting for transfers between devices, exchange(): return lax.all_to_all(value, axes, 0, 0, tiled=True)  7.24 us
    ppermute x1, waiting for transfers between devices, body(): partner = lax.ppermute(own, PAIR, [(0, 1), (1, 0)])  5 us
  transfers between devices with their start and end apart: 3, of which 2 were waited for; matrix products, arithmetic and copies ran while one was open for 0% of the time, Pallas kernels for 4%

profile of v1, /device:TPU:1, one launch (start us, length us, event | category | flops | bytes accessed | tf_op | source)
XLA Modules:
  0.0 121.0 jit_solution(9627171271222498663)
XLA Ops:
  0.6 1.7 %broadcast_in_dim.11 = bf16[8,128,256]{2,1,0:T(8,128)(2,1)} broadcast(bf16[128,256]{1,0:T(8,128)(2,1)} %bitcast.7), dimensions={1,2} | broadcast | bytes 589824 | tf_op jit(solution)/shard_map/broadcast_in_dim | solution.py:135
  2.3 0.0 copy-start.1
  2.3 10.4 %all-to-all-start = ((bf16[8,128,256]{2,1,0:T(8,128)(2,1)}), bf16[8,128,256]{2,1,0:T(8,128)(2,1)S(1)}, u32[]{:S(2)}, u32[]{:S(2)}) async-start(bf16[8,128,256]{2,1,0:T(8,128)(2,1)} %broadcast_in_dim.11), calls=%async_computation | async-start | bytes 1048576 | tf_op jit(solution)/shard_map/all_to_all | solution.py:125
  12.7 0.0 copy-done.1
  12.7 1.9 %collective-permute-start = (bf16[128,256]{1,0:T(8,128)(2,1)S(1)}, bf16[128,256]{1,0:T(8,128)(2,1)S(1)}, u32[]{:S(2)}, u32[]{:S(2)}) collective-permute-start(bf16[128,256]{1,0:T(8,128)(2,1)S(1)} %bitcast.9), channel_id=1, source_target_pairs={{0,256},{256,0},{1,257},{257,1},{2,258},{258,2},{3,259},{259,3},{4... | collective-permute-start | bytes 196616 | tf_op jit(solution)/shard_map/ppermute | solution.py:134
  14.6 5.0 %collective-permute-done.partner_ref = bf16[128,256]{1,0:T(8,128)(2,1)S(1)} collective-permute-done((bf16[128,256]{1,0:T(8,128)(2,1)S(1)}, bf16[128,256]{1,0:T(8,128)(2,1)S(1)}, u32[]{:S(2)}, u32[]{:S(2)}) %collective-permute-start) | collective-permute-done | bytes 65568 | tf_op jit(solution)/shard_map/ppermute | solution.py:134
  19.6 0.0 copy-start.2
  19.6 28.9 %all_gather.3.col_ref = bf16[1024,256]{1,0:T(8,128)(2,1)} all-gather(bf16[128,256]{1,0:T(8,128)(2,1)S(1)} %collective-permute-done.partner_ref), channel_id=1, replica_groups=mesh['pair'=2,'rest'=4,'xh'=2,'zp'=8,'z0'=2,'core'=2] {'zp'}, dimensions={0}, use_global_device_ids=true | all-gather | bytes 589824 | tf_op jit(solution)/shard_map/all_gather | solution.py:137
  48.5 0.0 copy-done.2
  48.5 0.0 all-to-all-done
  48.5 0.0 copy-start
  48.5 0.8 copy-done
  49.3 4.6 %shard_map.49 = (f32[8,8,128]{2,1,0:T(8,128)}, f32[8,8,128]{2,1,0:T(8,128)}) custom-call(bf16[1024,256]{1,0:T(8,128)(2,1)} %bitcast.3, bf16[1024,256]{1,0:T(8,128)(2,1)} %all_gather.3.col_ref), custom_call_target="tpu_custom_call" | custom-call | flops 1073741824 | bytes 1114112 | tf_op jit(solution)/shard_map/pallas_call | solution.py:112
  54.0 18.5 %all_to_all.20.parts_ref = f32[8,8,128]{2,1,0:T(8,128)} all-to-all(f32[8,8,128]{2,1,0:T(8,128)} %get-tuple-element.10), channel_id=1, replica_groups=mesh['pair'=2,'rest'=4,'xh'=2,'zp'=8,'z0'=2,'core'=2] {'xh','z0','core'}, dimensions={0} | all-to-all | bytes 65536 | tf_op jit(solution)/shard_map/all_to_all | solution.py:125
  72.4 7.4 %all-to-all-start.1 = ((f32[8,8,128]{2,1,0:T(8,128)}), f32[8,8,128]{2,1,0:T(8,128)S(1)}, u32[]{:S(2)}, u32[]{:S(2)}) async-start(f32[8,8,128]{2,1,0:T(8,128)} %get-tuple-element.9), calls=%async_computation.1 | async-start | bytes 65536 | tf_op jit(solution)/shard_map/all_to_all | solution.py:125
  79.9 4.4 %shard_map.50 = (f32[8,128,256]{2,1,0:T(8,128)}, f32[1,128]{1,0:T(1,128)}, f32[1,128]{1,0:T(1,128)}, f32[128,256]{1,0:T(8,128)}) custom-call(bf16[1024,256]{1,0:T(8,128)(2,1)} %bitcast.4, bf16[1024,256]{1,0:T(8,128)(2,1)} %all_gather.3.col_ref, f32[8,8,128]{2,1,0:T(8,128)} %all_to_all.20.parts_ref, bf16[128,256]{1,0:T(8,128)(2,1)} %bitcast.8, ...), custom_call_target="tpu_custom_call" | custom-call | flops 1073741824 | bytes 2397184 | tf_op jit(solution)/shard_map/pallas_call | solution.py:112
  84.3 7.2 %all-to-all-done.1.parts_ref = f32[8,8,128]{2,1,0:T(8,128)S(1)} async-done(((f32[8,8,128]{2,1,0:T(8,128)}), f32[8,8,128]{2,1,0:T(8,128)S(1)}, u32[]{:S(2)}, u32[]{:S(2)}) %all-to-all-start.1) | async-done | bytes 32800 | tf_op jit(solution)/shard_map/all_to_all | solution.py:125
  91.5 0.0 copy-start.3
  91.5 0.6 copy-done.3
  92.2 4.8 %shard_map.51 = f32[8,128,256]{2,1,0:T(8,128)} custom-call(bf16[1024,256]{1,0:T(8,128)(2,1)} %bitcast.5, bf16[1024,256]{1,0:T(8,128)(2,1)} %all_gather.3.col_ref, f32[8,8,128]{2,1,0:T(8,128)} %copy-done.3, f32[8,128,256]{2,1,0:T(8,128)} %get-tuple-element.11.own_grad_ref), custom_call_target="tpu_custom_call" | custom-call | flops 1073741824 | bytes 3178496 | tf_op jit(solution)/shard_map/pallas_call | solution.py:112
  96.9 22.1 %all_to_all.21.parts_ref = f32[8,128,256]{2,1,0:T(8,128)} all-to-all(f32[8,128,256]{2,1,0:T(8,128)} %shard_map.51), channel_id=1, replica_groups=mesh['pair'=2,'rest'=4,'xh'=2,'zp'=8,'z0'=2,'core'=2] {'xh','z0','core'}, dimensions={0} | all-to-all | bytes 2097152 | tf_op jit(solution)/shard_map/all_to_all | solution.py:125
  119.1 1.9 %shard_map.52 = f32[128,256]{1,0:T(8,128)} custom-call(f32[8,128,256]{2,1,0:T(8,128)} %all_to_all.21.parts_ref, f32[128,256]{1,0:T(8,128)} %get-tuple-element.12.base_ref), custom_call_target="tpu_custom_call" | custom-call | bytes 1310720 | tf_op jit(solution)/shard_map/pallas_call | solution.py:112
Async XLA Ops:
  2.3 10.4 %copy-start.1 = (bf16[1,128,256]{2,1,0:T(8,128)(2,1)S(1)}, bf16[1,128,256]{2,1,0:T(8,128)(2,1)}, u32[]{:S(2)}) copy-start(bf16[1,128,256]{2,1,0:T(8,128)(2,1)} %param.2) | copy-start | bytes 196612
  2.3 46.2 %all-to-all-start = ((bf16[8,128,256]{2,1,0:T(8,128)(2,1)}), bf16[8,128,256]{2,1,0:T(8,128)(2,1)S(1)}, u32[]{:S(2)}, u32[]{:S(2)}) async-start(bf16[8,128,256]{2,1,0:T(8,128)(2,1)} %broadcast_in_dim.11), calls=%async_computation | async-start | bytes 1048576 | tf_op jit(solution)/shard_map/all_to_all | solution.py:125
  12.7 6.9 %collective-permute-start = (bf16[128,256]{1,0:T(8,128)(2,1)S(1)}, bf16[128,256]{1,0:T(8,128)(2,1)S(1)}, u32[]{:S(2)}, u32[]{:S(2)}) collective-permute-start(bf16[128,256]{1,0:T(8,128)(2,1)S(1)} %bitcast.9), channel_id=1, source_target_pairs={{0,256},{256,0},{1,257},{257,1},{2,258},{258,2},{3,259},{259,3},{4... | collective-permute-start | bytes 196616 | tf_op jit(solution)/shard_map/ppermute | solution.py:134
  19.6 28.9 %copy-start.2 = (bf16[128,256]{1,0:T(8,128)(2,1)}, bf16[128,256]{1,0:T(8,128)(2,1)S(1)}, u32[]{:S(2)}) copy-start(bf16[128,256]{1,0:T(8,128)(2,1)S(1)} %collective-permute-done.partner_ref) | copy-start | bytes 196612
  48.5 0.8 copy-start
  72.4 19.1 %all-to-all-start.1 = ((f32[8,8,128]{2,1,0:T(8,128)}), f32[8,8,128]{2,1,0:T(8,128)S(1)}, u32[]{:S(2)}, u32[]{:S(2)}) async-start(f32[8,8,128]{2,1,0:T(8,128)} %get-tuple-element.9), calls=%async_computation.1 | async-start | bytes 65536 | tf_op jit(solution)/shard_map/all_to_all | solution.py:125
  91.5 0.6 copy-start.3

commit v2 on v1

--- a/solution.py
+++ b/solution.py
@@ -4,6 +4,7 @@
 from jax.experimental import pallas as pl
 from jax.experimental.pallas import tpu as pltpu
 from jax.sharding import Mesh, PartitionSpec as P
+
 
 logit_scale = 10.0
 
@@ -42,8 +43,11 @@
             total = total + jnp.sum(block.reshape(step // 8, 8, width), axis=0)
         lse = top + jnp.log(jnp.sum(total, axis=0, keepdims=True))
         tile = jnp.concatenate([lse[:, i : i + 128] for i in range(0, width, 128)], axis=0)
-        for peer in range(out.shape[0]):
-            out[peer] = tile
+        if len(out.shape) == 2:
+            out[...] = tile
+        else:
+            for peer in range(out.shape[0]):
+                out[peer] = tile
 
 
 def own_kernel(
@@ -115,6 +119,7 @@
         in_specs=[VMEM] * len(args),
         out_specs=VMEM if single else tuple([VMEM] * len(out_list)),
         scratch_shapes=list(scratch),
+        compiler_params=pltpu.CompilerParams(vmem_limit_bytes=16 << 20),
         cost_estimate=pl.CostEstimate(
             flops=flops, bytes_accessed=moved, transcendentals=transcendentals
         ),
@@ -125,7 +130,7 @@
     return lax.all_to_all(value, axes, 0, 0, tiled=True)
 
 
-def body(embeddings, positive):
+def step(embeddings, positive):
     own = embeddings[0]
     row_count, width = own.shape
     rows_n = lax.axis_size(XH) * lax.axis_size(Z0) * lax.axis_size(CORE)
@@ -140,14 +145,14 @@
     row_parts, col_parts = call(
         lse_kernel,
         (
-            jax.ShapeDtypeStruct((rows_n, rows_total // 128, 128), f32),
+            jax.ShapeDtypeStruct((rows_total // 128, 128), f32),
             jax.ShapeDtypeStruct((cols_n, cols_total // 128, 128), f32),
         ),
         rows, cols,
         flops=4 * area * width, transcendentals=2 * area,
         scratch=[pltpu.VMEM((max(rows_total, cols_total),) * 2, f32)],
     )
-    row_parts = exchange(row_parts, ROW_GROUP)
+    row_parts = lax.all_gather(row_parts, ROW_GROUP, axis=0, tiled=False)
     col_parts = exchange(col_parts, COL_GROUP)
     grads, totals, row_loss, base = call(
         own_kernel,
@@ -179,7 +184,7 @@
     )
     v, b = (PAIR, REST), (XH, ZP, Z0, CORE)
     return jax.shard_map(
-        body,
+        step,
         mesh=inner,
         in_specs=(P(v, b, None), P(None, b)),
         out_specs=(P(v, b, None), P(v, b), P(v, b)),

time: 122 us -> 107 us (0.88)
  Pallas kernels: 15.8 us -> 8.42 us
  waiting for transfers between devices: 12.2 us -> 5 us
  local copies, waits for them, and re-layouts: 3.08 us -> 1.69 us
    all_gather x1 -> x2, blocking collectives: 28.9 us -> 49.5 us  [the longest x1 27 us: step(): cols = lax.all_gather(partner, COL_GROUP, axis=0, tiled=True)]
    all_to_all x2 -> x1, blocking collectives: 40.6 us -> 21.2 us  [exchange(): return lax.all_to_all(value, axes, 0, 0, tiled=True)]
    pallas_call x4, Pallas kernels: 15.8 us -> 8.42 us  [call(): pl.pallas_call(kernel, out_shape=outs, in_specs=[VMEM] * len(args), out_s...]
    all_to_all x2, waiting for transfers between devices: 7.24 us -> 0.01 us  [exchange(): return lax.all_to_all(value, axes, 0, 0, tiled=True)]
    unnamed x8 -> x4, local copies, waits for them, and re-layouts: 1.41 us -> 0.01 us
  transfers between devices with their start and end apart: 3 -> 3, of which waited for: 2 -> 1; matrix products, arithmetic and copies ran while one was open for 0% -> 0% of each run, Pallas kernels for 4% -> 3%
where the time goes in v2:
time: 107 us; the launch traced here: 106 us
  blocking collectives  70.7 us (66%)
  starting transfers between devices  19.7 us (18%)
  Pallas kernels  8.42 us (8%)
  waiting for transfers between devices  5 us (5%)
  local copies, waits for them, and re-layouts  1.69 us (2%)
    all_gather x1, blocking collectives, step(): cols = lax.all_gather(partner, COL_GROUP, axis=0, tiled=True)  27 us
    all_gather x1, blocking collectives, step(): row_parts = lax.all_gather(row_parts, ROW_GROUP, axis=0, tiled=False)  22.5 us
    all_to_all x1, blocking collectives, exchange(): return lax.all_to_all(value, axes, 0, 0, tiled=True)  21.2 us
    all_to_all x2, starting transfers between devices, exchange(): return lax.all_to_all(value, axes, 0, 0, tiled=True)  17.8 us
    pallas_call x4, Pallas kernels, call(): pl.pallas_call(kernel, out_shape=outs, in_specs=[VMEM] * len(args), out_s...  8.42 us
    ppermute x1, waiting for transfers between devices, step(): partner = lax.ppermute(own, PAIR, [(0, 1), (1, 0)])  5 us
  transfers between devices with their start and end apart: 3, of which 1 were waited for; matrix products, arithmetic and copies ran while one was open for 0% of the time, Pallas kernels for 3%

profile of v2, /device:TPU:1, one launch (start us, length us, event | category | flops | bytes accessed | tf_op | source)
XLA Modules:
  0.0 106.1 jit_solution(14147353723816913706)
XLA Ops:
  0.6 1.7 %broadcast_in_dim.11 = bf16[8,128,256]{2,1,0:T(8,128)(2,1)} broadcast(bf16[128,256]{1,0:T(8,128)(2,1)} %bitcast.7), dimensions={1,2} | broadcast | bytes 589824 | tf_op jit(solution)/shard_map/broadcast_in_dim | solution.py:140
  2.3 0.0 copy-start
  2.3 10.4 %all-to-all-start = ((bf16[8,128,256]{2,1,0:T(8,128)(2,1)}), bf16[8,128,256]{2,1,0:T(8,128)(2,1)S(1)}, u32[]{:S(2)}, u32[]{:S(2)}) async-start(bf16[8,128,256]{2,1,0:T(8,128)(2,1)} %broadcast_in_dim.11), calls=%async_computation | async-start | bytes 1048576 | tf_op jit(solution)/shard_map/all_to_all | solution.py:130
  12.7 0.0 copy-done
  12.7 1.9 %collective-permute-start = (bf16[128,256]{1,0:T(8,128)(2,1)S(1)}, bf16[128,256]{1,0:T(8,128)(2,1)S(1)}, u32[]{:S(2)}, u32[]{:S(2)}) collective-permute-start(bf16[128,256]{1,0:T(8,128)(2,1)S(1)} %bitcast.8), channel_id=1, source_target_pairs={{0,256},{256,0},{1,257},{257,1},{2,258},{258,2},{3,259},{259,3},{4... | collective-permute-start | bytes 196616 | tf_op jit(solution)/shard_map/ppermute | solution.py:139
  14.6 5.0 %collective-permute-done.partner_ref = bf16[128,256]{1,0:T(8,128)(2,1)S(1)} collective-permute-done((bf16[128,256]{1,0:T(8,128)(2,1)S(1)}, bf16[128,256]{1,0:T(8,128)(2,1)S(1)}, u32[]{:S(2)}, u32[]{:S(2)}) %collective-permute-start) | collective-permute-done | bytes 65568 | tf_op jit(solution)/shard_map/ppermute | solution.py:139
  19.6 27.0 %all_gather.9.col_ref = bf16[1024,256]{1,0:T(8,128)(2,1)S(1)} all-gather(bf16[128,256]{1,0:T(8,128)(2,1)S(1)} %collective-permute-done.partner_ref), channel_id=1, replica_groups=mesh['pair'=2,'rest'=4,'xh'=2,'zp'=8,'z0'=2,'core'=2] {'zp'}, dimensions={0}, use_global_device_ids=true | all-gather | bytes 589824 | tf_op jit(solution)/shard_map/all_gather | solution.py:142
  46.6 0.0 all-to-all-done
  46.6 2.8 %shard_map.49 = (f32[8,128]{1,0:T(8,128)S(1)}, f32[8,8,128]{2,1,0:T(8,128)}) custom-call(bf16[1024,256]{1,0:T(8,128)(2,1)S(1)} %bitcast.4, bf16[1024,256]{1,0:T(8,128)(2,1)S(1)} %all_gather.9.col_ref), custom_call_target="tpu_custom_call" | custom-call | flops 1073741824 | bytes 1085440 | tf_op jit(solution)/shard_map/pallas_call | solution.py:116
  49.4 7.4 %all-to-all-start.1 = ((f32[8,8,128]{2,1,0:T(8,128)}), f32[8,8,128]{2,1,0:T(8,128)S(1)}, u32[]{:S(2)}, u32[]{:S(2)}) async-start(f32[8,8,128]{2,1,0:T(8,128)} %get-tuple-element.9), calls=%async_computation.1 | async-start | bytes 65536 | tf_op jit(solution)/shard_map/all_to_all | solution.py:130
  56.9 0.0 copy-start.1
  56.9 22.5 %all-gather = f32[64,128]{1,0:T(8,128)S(1)} all-gather(f32[8,128]{1,0:T(8,128)S(1)} %get-tuple-element.10), channel_id=2, replica_groups=mesh['pair'=2,'rest'=4,'xh'=2,'zp'=8,'z0'=2,'core'=2] {'xh','z0','core'}, dimensions={0}, use_global_device_ids=true | all-gather | bytes 36864 | tf_op jit(solution)/shard_map/all_gather | solution.py:155
  79.4 0.0 copy-done.1
  79.4 2.7 %shard_map.50 = (f32[8,128,256]{2,1,0:T(8,128)S(1)}, f32[1,128]{1,0:T(1,128)}, f32[1,128]{1,0:T(1,128)}, f32[128,256]{1,0:T(8,128)S(1)}) custom-call(bf16[1024,256]{1,0:T(8,128)(2,1)S(1)} %bitcast.5, bf16[1024,256]{1,0:T(8,128)(2,1)S(1)} %all_gather.9.col_ref, f32[8,8,128]{2,1,0:T(8,128)S(1)} %bitcast.10, bf16[128,256]{1,0:T(8,128)(2,1)S(1)} %bitcast.9, ...), custom_call_target="tpu_custom_call" | custom-call | flops 1073741824 | bytes 2397184 | tf_op jit(solution)/shard_map/pallas_call | solution.py:116
  82.0 0.0 all-to-all-done.1.parts_ref
  82.0 2.2 %shard_map.51 = f32[8,128,256]{2,1,0:T(8,128)S(1)} custom-call(bf16[1024,256]{1,0:T(8,128)(2,1)S(1)} %bitcast.6, bf16[1024,256]{1,0:T(8,128)(2,1)S(1)} %all_gather.9.col_ref, f32[8,8,128]{2,1,0:T(8,128)S(1)} %all-to-all-done.1.parts_ref, f32[8,128,256]{2,1,0:T(8,128)S(1)} %get-tuple-element.11.own_grad_ref), custom_call_target="tpu_custom_call" | custom-call | flops 1073741824 | bytes 3178496 | tf_op jit(solution)/shard_map/pallas_call | solution.py:116
  84.3 21.2 %all_to_all.15.parts_ref = f32[8,128,256]{2,1,0:T(8,128)S(1)} all-to-all(f32[8,128,256]{2,1,0:T(8,128)S(1)} %shard_map.51), channel_id=1, replica_groups=mesh['pair'=2,'rest'=4,'xh'=2,'zp'=8,'z0'=2,'core'=2] {'xh','z0','core'}, dimensions={0} | all-to-all | bytes 2097152 | tf_op jit(solution)/shard_map/all_to_all | solution.py:130
  105.4 0.7 shard_map.52
Async XLA Ops:
  2.3 10.4 %copy-start = (bf16[1,128,256]{2,1,0:T(8,128)(2,1)S(1)}, bf16[1,128,256]{2,1,0:T(8,128)(2,1)}, u32[]{:S(2)}) copy-start(bf16[1,128,256]{2,1,0:T(8,128)(2,1)} %param.2) | copy-start | bytes 196612
  2.3 44.3 %all-to-all-start = ((bf16[8,128,256]{2,1,0:T(8,128)(2,1)}), bf16[8,128,256]{2,1,0:T(8,128)(2,1)S(1)}, u32[]{:S(2)}, u32[]{:S(2)}) async-start(bf16[8,128,256]{2,1,0:T(8,128)(2,1)} %broadcast_in_dim.11), calls=%async_computation | async-start | bytes 1048576 | tf_op jit(solution)/shard_map/all_to_all | solution.py:130
  12.7 6.9 %collective-permute-start = (bf16[128,256]{1,0:T(8,128)(2,1)S(1)}, bf16[128,256]{1,0:T(8,128)(2,1)S(1)}, u32[]{:S(2)}, u32[]{:S(2)}) collective-permute-start(bf16[128,256]{1,0:T(8,128)(2,1)S(1)} %bitcast.8), channel_id=1, source_target_pairs={{0,256},{256,0},{1,257},{257,1},{2,258},{258,2},{3,259},{259,3},{4... | collective-permute-start | bytes 196616 | tf_op jit(solution)/shard_map/ppermute | solution.py:139
  49.4 32.6 %all-to-all-start.1 = ((f32[8,8,128]{2,1,0:T(8,128)}), f32[8,8,128]{2,1,0:T(8,128)S(1)}, u32[]{:S(2)}, u32[]{:S(2)}) async-start(f32[8,8,128]{2,1,0:T(8,128)} %get-tuple-element.9), calls=%async_computation.1 | async-start | bytes 65536 | tf_op jit(solution)/shard_map/all_to_all | solution.py:130
  56.9 22.5 %copy-start.1 = (s32[8,128]{1,0:T(8,128)S(1)}, s32[8,128]{1,0:T(8,128)}, u32[]{:S(2)}) copy-start(s32[8,128]{1,0:T(8,128)} %positive_ref.1) | copy-start | bytes 12292

commit v3 on v2

--- a/solution.py
+++ b/solution.py
@@ -1,3 +1,5 @@
+import functools
+
 import jax
 import jax.numpy as jnp
 from jax import lax
@@ -54,7 +56,8 @@
     row_ref, col_ref, parts_ref, own_ref, partner_ref, positive_ref,
     grad_ref, totals_ref, loss_ref, base_ref, totals_scratch,
 ):
-    totals = combine(parts_ref[...])
+    groups, halves, tile_rows, lanes = parts_ref.shape
+    totals = combine(parts_ref[...].reshape(groups * halves, tile_rows, lanes))
     totals_scratch[...] = totals
     block_rows = totals.shape[1]
     width = col_ref.shape[0]
@@ -89,14 +92,18 @@
     loss_ref[...] = own_totals - pos_score
 
 
-def side_kernel(row_ref, col_ref, parts_ref, own_grad_ref, grad_ref):
+def side_kernel(flip, row_ref, col_ref, parts_ref, own_grad_ref, grad_ref):
     totals = combine(parts_ref[...])
     shift = jnp.concatenate([totals[i : i + 1, :] for i in range(totals.shape[0])], axis=1)
     block_rows = grad_ref.shape[1]
+    cores = lax.axis_size(CORE)
+    core = lax.rem(lax.axis_index(CORE) + flip, cores)
     for i in range(grad_ref.shape[0]):
-        scores = score_block(row_ref[i * block_rows : (i + 1) * block_rows, :], col_ref[...])
+        block = i * cores + core
+        start = pl.multiple_of(block * block_rows, block_rows)
+        scores = score_block(row_ref[pl.ds(start, block_rows), :], col_ref[...])
         weights = jnp.exp(scores - shift)
-        grad_ref[i] = own_grad_ref[i] + jnp.dot(
+        grad_ref[i] = own_grad_ref[block] + jnp.dot(
             weights.astype(jnp.bfloat16), col_ref[...], preferred_element_type=jnp.float32
         )
 
@@ -152,7 +159,8 @@
         flops=4 * area * width, transcendentals=2 * area,
         scratch=[pltpu.VMEM((max(rows_total, cols_total),) * 2, f32)],
     )
-    row_parts = lax.all_gather(row_parts, ROW_GROUP, axis=0, tiled=False)
+    far_parts = lax.ppermute(row_parts, Z0, [(0, 1), (1, 0)])
+    row_parts = lax.all_gather(jnp.stack([row_parts, far_parts]), (XH, CORE), axis=0, tiled=False)
     col_parts = exchange(col_parts, COL_GROUP)
     grads, totals, row_loss, base = call(
         own_kernel,
@@ -166,13 +174,17 @@
         flops=4 * area * width, transcendentals=area,
         scratch=[pltpu.VMEM((rows_total // 128, 128), f32)],
     )
-    grads = call(
-        side_kernel,
-        jax.ShapeDtypeStruct((rows_n, row_count, width), f32),
-        rows, cols, col_parts, grads,
-        flops=4 * area * width, transcendentals=area,
-    )
-    grads = exchange(grads, ROW_GROUP)
+    halves = [
+        call(
+            functools.partial(side_kernel, flip),
+            jax.ShapeDtypeStruct((rows_n // 2, row_count, width), f32),
+            rows, cols, col_parts, grads,
+            flops=2 * area * width, transcendentals=area // 2,
+        )
+        for flip in (1, 0)
+    ]
+    received = lax.ppermute(halves[0], CORE, [(0, 1), (1, 0)])
+    grads = exchange(halves[1] + received, (XH, Z0))
     gradients = call(sum_kernel, jax.ShapeDtypeStruct((row_count, width), f32), grads, base)
     return (gradients[None], totals, row_loss)
 

time: 107 us -> 100 us (0.935)
  blocking collectives: 70.7 us -> 53.4 us
  starting transfers between devices: 19.7 us -> 29.2 us
    ppermute x0 -> x2, starting transfers between devices: none -> 9.72 us  [the longest x1 5.6 us: step(): received = lax.ppermute(halves[0], CORE, [(0, 1), (1, 0)])]
    all_gather x1, blocking collectives: 22.5 us -> 13.5 us  [step(): lax.all_gather(jnp.stack([row_parts, far_parts]), (XH, CORE), axis=0, til...]
    all_to_all x1, blocking collectives: 21.2 us -> 12.9 us  [exchange(): return lax.all_to_all(value, axes, 0, 0, tiled=True)]
    pallas_call x4 -> x5, Pallas kernels: 8.42 us -> 8.68 us  [call(): pl.pallas_call(kernel, out_shape=outs, in_specs=[VMEM] * len(args), out_s...]
  transfers between devices with their start and end apart: 3 -> 5, of which waited for: 1 -> 2; matrix products, arithmetic and copies ran while one was open for 0% -> 0% of each run, Pallas kernels for 3% -> 4%
where the time goes in v3:
time: 100 us; the launch traced here: 99 us
  blocking collectives  53.4 us (53%)
  starting transfers between devices  29.2 us (29%)
  Pallas kernels  8.68 us (9%)
  waiting for transfers between devices  5.26 us (5%)
  local copies, waits for them, and re-layouts  1.68 us (2%)
    all_gather x1, blocking collectives, step(): cols = lax.all_gather(partner, COL_GROUP, axis=0, tiled=True)  27 us
    all_to_all x2, starting transfers between devices, exchange(): return lax.all_to_all(value, axes, 0, 0, tiled=True)  17.6 us
    all_gather x1, blocking collectives, step(): lax.all_gather(jnp.stack([row_parts, far_parts]), (XH, CORE), axis=0, til...  13.5 us
    all_to_all x1, blocking collectives, exchange(): return lax.all_to_all(value, axes, 0, 0, tiled=True)  12.9 us
    pallas_call x5, Pallas kernels, call(): pl.pallas_call(kernel, out_shape=outs, in_specs=[VMEM] * len(args), out_s...  8.68 us
    ppermute x1, starting transfers between devices, step(): received = lax.ppermute(halves[0], CORE, [(0, 1), (1, 0)])  5.6 us
    ppermute x1, waiting for transfers between devices, step(): partner = lax.ppermute(own, PAIR, [(0, 1), (1, 0)])  5 us
    ppermute x1, starting transfers between devices, step(): far_parts = lax.ppermute(row_parts, Z0, [(0, 1), (1, 0)])  4.13 us
  transfers between devices with their start and end apart: 5, of which 2 were waited for; matrix products, arithmetic and copies ran while one was open for 0% of the time, Pallas kernels for 4%

profile of v3, /device:TPU:1, one launch (start us, length us, event | category | flops | bytes accessed | tf_op | source)
XLA Modules:
  0.0 99.0 jit_solution(10273305813374034771)
XLA Ops:
  0.6 1.7 %broadcast_in_dim.11 = bf16[8,128,256]{2,1,0:T(8,128)(2,1)} broadcast(bf16[128,256]{1,0:T(8,128)(2,1)} %bitcast.10), dimensions={1,2} | broadcast | bytes 589824 | tf_op jit(solution)/shard_map/broadcast_in_dim | solution.py:147
  2.3 0.0 copy-start
  2.3 10.4 %all-to-all-start = ((bf16[8,128,256]{2,1,0:T(8,128)(2,1)}), bf16[8,128,256]{2,1,0:T(8,128)(2,1)S(1)}, u32[]{:S(2)}, u32[]{:S(2)}) async-start(bf16[8,128,256]{2,1,0:T(8,128)(2,1)} %broadcast_in_dim.11), calls=%async_computation | async-start | bytes 1048576 | tf_op jit(solution)/shard_map/all_to_all | solution.py:137
  12.7 0.0 copy-done
  12.7 1.9 %collective-permute-start = (bf16[128,256]{1,0:T(8,128)(2,1)S(1)}, bf16[128,256]{1,0:T(8,128)(2,1)S(1)}, u32[]{:S(2)}, u32[]{:S(2)}) collective-permute-start(bf16[128,256]{1,0:T(8,128)(2,1)S(1)} %bitcast.11), channel_id=1, source_target_pairs={{0,256},{256,0},{1,257},{257,1},{2,258},{258,2},{3,259},{259,3},{4... | collective-permute-start | bytes 196616 | tf_op jit(solution)/shard_map/ppermute | solution.py:146
  14.6 5.0 %collective-permute-done.partner_ref = bf16[128,256]{1,0:T(8,128)(2,1)S(1)} collective-permute-done((bf16[128,256]{1,0:T(8,128)(2,1)S(1)}, bf16[128,256]{1,0:T(8,128)(2,1)S(1)}, u32[]{:S(2)}, u32[]{:S(2)}) %collective-permute-start) | collective-permute-done | bytes 65568 | tf_op jit(solution)/shard_map/ppermute | solution.py:146
  19.6 27.0 %all_gather.9.col_ref = bf16[1024,256]{1,0:T(8,128)(2,1)S(1)} all-gather(bf16[128,256]{1,0:T(8,128)(2,1)S(1)} %collective-permute-done.partner_ref), channel_id=1, replica_groups=mesh['pair'=2,'rest'=4,'xh'=2,'zp'=8,'z0'=2,'core'=2] {'zp'}, dimensions={0}, use_global_device_ids=true | all-gather | bytes 589824 | tf_op jit(solution)/shard_map/all_gather | solution.py:149
  46.6 0.0 all-to-all-done
  46.6 2.8 %shard_map.49 = (f32[8,128]{1,0:T(8,128)S(1)}, f32[8,8,128]{2,1,0:T(8,128)}) custom-call(bf16[1024,256]{1,0:T(8,128)(2,1)S(1)} %bitcast.6, bf16[1024,256]{1,0:T(8,128)(2,1)S(1)} %all_gather.9.col_ref), custom_call_target="tpu_custom_call" | custom-call | flops 1073741824 | bytes 1085440 | tf_op jit(solution)/shard_map/pallas_call | solution.py:123
  49.4 4.1 %collective-permute-start.1 = (f32[8,128]{1,0:T(8,128)S(1)}, f32[8,128]{1,0:T(8,128)S(1)}, u32[]{:S(2)}, u32[]{:S(2)}) collective-permute-start(f32[8,128]{1,0:T(8,128)S(1)} %get-tuple-element.10), channel_id=1, source_target_pairs={{0,2},{2,0},{1,3},{3,1},{4,6},{6,4},{5,7},{7,5},{8,10},{10,8},{9,1... | collective-permute-start | bytes 12296 | tf_op jit(solution)/shard_map/ppermute | solution.py:162
  53.6 7.2 %all-to-all-start.1 = ((f32[8,8,128]{2,1,0:T(8,128)}), f32[8,8,128]{2,1,0:T(8,128)S(1)}, u32[]{:S(2)}, u32[]{:S(2)}) async-start(f32[8,8,128]{2,1,0:T(8,128)} %get-tuple-element.9), calls=%async_computation.1 | async-start | bytes 65536 | tf_op jit(solution)/shard_map/all_to_all | solution.py:137
  60.8 0.0 collective-permute-done.1
  60.8 0.0 copy-start.1
  60.8 13.5 %all-gather = f32[8,8,128]{2,1,0:T(8,128)S(1)} all-gather(f32[2,8,128]{2,1,0:T(8,128)S(1)} %pad_maximum_fusion), channel_id=2, replica_groups=mesh['pair'=2,'rest'=4,'xh'=2,'zp'=8,'z0'=2,'core'=2] {'xh','core'}, dimensions={0}, use_global_device_ids=true | all-gather | bytes 40960 | tf_op jit(solution)/shard_map/all_gather | solution.py:163
  74.3 0.0 copy-done.1
  74.3 2.7 %shard_map.50 = (f32[8,128,256]{2,1,0:T(8,128)S(1)}, f32[1,128]{1,0:T(1,128)}, f32[1,128]{1,0:T(1,128)}, f32[128,256]{1,0:T(8,128)S(1)}) custom-call(bf16[1024,256]{1,0:T(8,128)(2,1)S(1)} %bitcast.7, bf16[1024,256]{1,0:T(8,128)(2,1)S(1)} %all_gather.9.col_ref, f32[4,2,8,128]{3,2,1,0:T(8,128)S(1)} %bitcast.13, bf16[128,256]{1,0:T(8,128)(2,1)S(1)} %bitcast.12, ...), custom_call_target="tpu_custom_call" | custom-call | flops 1073741824 | bytes 2397184 | tf_op jit(solution)/shard_map/pallas_call | solution.py:123
  77.0 0.0 all-to-all-done.1.parts_ref
  77.0 1.2 %shard_map.52 = f32[4,128,256]{2,1,0:T(8,128)S(1)} custom-call(bf16[1024,256]{1,0:T(8,128)(2,1)S(1)} %bitcast.8, bf16[1024,256]{1,0:T(8,128)(2,1)S(1)} %all_gather.9.col_ref, f32[8,8,128]{2,1,0:T(8,128)S(1)} %all-to-all-done.1.parts_ref, f32[8,128,256]{2,1,0:T(8,128)S(1)} %get-tuple-element.11.own_grad_ref), custom_call_target="tpu_custom_call" | custom-call | flops 536870912 | bytes 2654208 | tf_op jit(solution)/shard_map/pallas_call | solution.py:123
  78.3 5.6 %collective-permute-start.2 = (f32[4,128,256]{2,1,0:T(8,128)S(1)}, f32[4,128,256]{2,1,0:T(8,128)S(1)}, u32[]{:S(2)}, u32[]{:S(2)}) collective-permute-start(f32[4,128,256]{2,1,0:T(8,128)S(1)} %shard_map.52), channel_id=1, source_target_pairs={{0,1},{1,0},{2,3},{3,2},{4,5},{5,4},{6,7},{7,6},{8,9},{9,8},{10,11... | collective-permute-start | bytes 1572872 | tf_op jit(solution)/shard_map/ppermute | solution.py:186
  83.9 1.3 %shard_map.51 = f32[4,128,256]{2,1,0:T(8,128)S(1)} custom-call(bf16[1024,256]{1,0:T(8,128)(2,1)S(1)} %bitcast.9, bf16[1024,256]{1,0:T(8,128)(2,1)S(1)} %all_gather.9.col_ref, f32[8,8,128]{2,1,0:T(8,128)S(1)} %all-to-all-done.1.parts_ref, f32[8,128,256]{2,1,0:T(8,128)S(1)} %get-tuple-element.11.own_grad_ref), custom_call_target="tpu_custom_call" | custom-call | flops 536870912 | bytes 2654208 | tf_op jit(solution)/shard_map/pallas_call | solution.py:123
  85.1 0.3 collective-permute-done.2
  85.4 0.1 add.3
  85.4 12.9 %all_to_all.15.parts_ref = f32[4,128,256]{2,1,0:T(8,128)S(1)} all-to-all(f32[4,128,256]{2,1,0:T(8,128)S(1)} %add.3), channel_id=1, replica_groups=mesh['pair'=2,'rest'=4,'xh'=2,'zp'=8,'z0'=2,'core'=2] {'xh','z0'}, dimensions={0} | all-to-all | bytes 1048576 | tf_op jit(solution)/shard_map/all_to_all | solution.py:137
  98.3 0.7 shard_map.53
  (1 shorter events, 0.0 us)
Async XLA Ops:
  2.3 10.4 %copy-start = (bf16[1,128,256]{2,1,0:T(8,128)(2,1)S(1)}, bf16[1,128,256]{2,1,0:T(8,128)(2,1)}, u32[]{:S(2)}) copy-start(bf16[1,128,256]{2,1,0:T(8,128)(2,1)} %param.2) | copy-start | bytes 196612
  2.3 44.3 %all-to-all-start = ((bf16[8,128,256]{2,1,0:T(8,128)(2,1)}), bf16[8,128,256]{2,1,0:T(8,128)(2,1)S(1)}, u32[]{:S(2)}, u32[]{:S(2)}) async-start(bf16[8,128,256]{2,1,0:T(8,128)(2,1)} %broadcast_in_dim.11), calls=%async_computation | async-start | bytes 1048576 | tf_op jit(solution)/shard_map/all_to_all | solution.py:137
  12.7 6.9 %collective-permute-start = (bf16[128,256]{1,0:T(8,128)(2,1)S(1)}, bf16[128,256]{1,0:T(8,128)(2,1)S(1)}, u32[]{:S(2)}, u32[]{:S(2)}) collective-permute-start(bf16[128,256]{1,0:T(8,128)(2,1)S(1)} %bitcast.11), channel_id=1, source_target_pairs={{0,256},{256,0},{1,257},{257,1},{2,258},{258,2},{3,259},{259,3},{4... | collective-permute-start | bytes 196616 | tf_op jit(solution)/shard_map/ppermute | solution.py:146
  49.4 11.3 %collective-permute-start.1 = (f32[8,128]{1,0:T(8,128)S(1)}, f32[8,128]{1,0:T(8,128)S(1)}, u32[]{:S(2)}, u32[]{:S(2)}) collective-permute-start(f32[8,128]{1,0:T(8,128)S(1)} %get-tuple-element.10), channel_id=1, source_target_pairs={{0,2},{2,0},{1,3},{3,1},{4,6},{6,4},{5,7},{7,5},{8,10},{10,8},{9,1... | collective-permute-start | bytes 12296 | tf_op jit(solution)/shard_map/ppermute | solution.py:162
  53.6 23.4 %all-to-all-start.1 = ((f32[8,8,128]{2,1,0:T(8,128)}), f32[8,8,128]{2,1,0:T(8,128)S(1)}, u32[]{:S(2)}, u32[]{:S(2)}) async-start(f32[8,8,128]{2,1,0:T(8,128)} %get-tuple-element.9), calls=%async_computation.1 | async-start | bytes 65536 | tf_op jit(solution)/shard_map/all_to_all | solution.py:137
  60.8 13.5 %copy-start.1 = (s32[8,128]{1,0:T(8,128)S(1)}, s32[8,128]{1,0:T(8,128)}, u32[]{:S(2)}) copy-start(s32[8,128]{1,0:T(8,128)} %positive_ref.1) | copy-start | bytes 12292
  78.3 7.1 %collective-permute-start.2 = (f32[4,128,256]{2,1,0:T(8,128)S(1)}, f32[4,128,256]{2,1,0:T(8,128)S(1)}, u32[]{:S(2)}, u32[]{:S(2)}) collective-permute-start(f32[4,128,256]{2,1,0:T(8,128)S(1)} %shard_map.52), channel_id=1, source_target_pairs={{0,1},{1,0},{2,3},{3,2},{4,5},{5,4},{6,7},{7,6},{8,9},{9,8},{10,11... | collective-permute-start | bytes 1572872 | tf_op jit(solution)/shard_map/ppermute | solution.py:186

commit v4 on v3

--- a/solution.py
+++ b/solution.py
@@ -9,24 +9,25 @@
 
 
 logit_scale = 10.0
+log2_e = 1.4426950408889634
+ln_2 = 0.6931471805599453
 
 PAIR, REST = "pair", "rest"
 XH, ZP, Z0, CORE = "xh", "zp", "z0", "core"
 ROW_GROUP = (XH, Z0, CORE)
-COL_GROUP = (ZP,)
+COL_GROUP = (ZP, CORE)
 VMEM = pl.BlockSpec(memory_space=pltpu.VMEM)
 
 
 def score_block(rows, cols):
-    return (
-        lax.dot_general(rows, cols, (((1,), (1,)), ((), ())), preferred_element_type=jnp.float32)
-        * logit_scale
-    )
+    return lax.dot_general(
+        rows, cols, (((1,), (1,)), ((), ())), preferred_element_type=jnp.float32
+    ) * (logit_scale * log2_e)
 
 
 def combine(parts):
     top = jnp.max(parts, axis=0)
-    return top + jnp.log(jnp.sum(jnp.exp(parts - top[None]), axis=0))
+    return top + jnp.log(jnp.sum(jnp.exp2(parts - top[None]), axis=0)) * log2_e
 
 
 def lse_kernel(row_ref, col_ref, row_lse_ref, col_lse_ref, score_ref):
@@ -41,9 +42,9 @@
         top = jnp.max(top, axis=0, keepdims=True)
         total = jnp.zeros((8, width), jnp.float32)
         for start in range(0, count, step):
-            block = jnp.exp(score_ref[start : start + step, :] - top)
+            block = jnp.exp2(score_ref[start : start + step, :] - top)
             total = total + jnp.sum(block.reshape(step // 8, 8, width), axis=0)
-        lse = top + jnp.log(jnp.sum(total, axis=0, keepdims=True))
+        lse = top + jnp.log(jnp.sum(total, axis=0, keepdims=True)) * log2_e
         tile = jnp.concatenate([lse[:, i : i + 128] for i in range(0, width, 128)], axis=0)
         if len(out.shape) == 2:
             out[...] = tile
@@ -64,7 +65,7 @@
     for i in range(totals.shape[0]):
         shift = jnp.broadcast_to(totals[i : i + 1, :], (128, block_rows)).T
         scores = score_block(row_ref[i * block_rows : (i + 1) * block_rows, :], col_ref[...])
-        weights = jnp.exp(scores - jnp.concatenate([shift] * (width // 128), axis=1))
+        weights = jnp.exp2(scores - jnp.concatenate([shift] * (width // 128), axis=1))
         grad_ref[i] = jnp.dot(
             weights.astype(jnp.bfloat16), col_ref[...], preferred_element_type=jnp.float32
         )
@@ -87,7 +88,7 @@
     pos_score = jnp.sum(product.T, axis=0, keepdims=True) * logit_scale
     place = (lax.axis_index(XH) * lax.axis_size(Z0) + lax.axis_index(Z0)) * lax.axis_size(CORE)
     place = place + lax.axis_index(CORE)
-    own_totals = totals_scratch[pl.ds(place, 1), :]
+    own_totals = totals_scratch[pl.ds(place, 1), :] * ln_2
     totals_ref[...] = own_totals
     loss_ref[...] = own_totals - pos_score
 
@@ -102,7 +103,7 @@
         block = i * cores + core
         start = pl.multiple_of(block * block_rows, block_rows)
         scores = score_block(row_ref[pl.ds(start, block_rows), :], col_ref[...])
-        weights = jnp.exp(scores - shift)
+        weights = jnp.exp2(scores - shift)
         grad_ref[i] = own_grad_ref[block] + jnp.dot(
             weights.astype(jnp.bfloat16), col_ref[...], preferred_element_type=jnp.float32
         )
@@ -133,8 +134,13 @@
     )(*args)
 
 
-def exchange(value, axes):
-    return lax.all_to_all(value, axes, 0, 0, tiled=True)
+def col_groups():
+    planes, cores = lax.axis_size(ZP), lax.axis_size(CORE)
+    return [[p * cores + (p + g) % cores for p in range(planes)] for g in range(cores)]
+
+
+def exchange(value, axes, groups=None):
+    return lax.all_to_all(value, axes, 0, 0, tiled=True, axis_index_groups=groups)
 
 
 def step(embeddings, positive):
@@ -146,7 +152,7 @@
     partner = lax.ppermute(own, PAIR, [(0, 1), (1, 0)])
     rows = exchange(jnp.broadcast_to(own[None], (rows_n, row_count, width)), ROW_GROUP)
     rows = rows.reshape(rows_n * row_count, width)
-    cols = lax.all_gather(partner, COL_GROUP, axis=0, tiled=True)
+    cols = lax.all_gather(partner, COL_GROUP, axis=0, tiled=True, axis_index_groups=col_groups())
     rows_total, cols_total = rows.shape[0], cols.shape[0]
     area = rows_total * cols_total
     row_parts, col_parts = call(
@@ -161,7 +167,7 @@
     )
     far_parts = lax.ppermute(row_parts, Z0, [(0, 1), (1, 0)])
     row_parts = lax.all_gather(jnp.stack([row_parts, far_parts]), (XH, CORE), axis=0, tiled=False)
-    col_parts = exchange(col_parts, COL_GROUP)
+    col_parts = exchange(col_parts, COL_GROUP, col_groups())
     grads, totals, row_loss, base = call(
         own_kernel,
         (

time: 100 us -> 97.1 us (0.971)
  starting transfers between devices: 29.2 us -> 26.7 us
  blocking collectives: 53.4 us -> 51 us
  waiting for transfers between devices: 5.26 us -> 6.84 us
    all_gather x1, blocking collectives: 13.5 us -> 7.48 us  [step(): lax.all_gather(jnp.stack([row_parts, far_parts]), (XH, CORE), axis=0, til...]
    all_gather x1, blocking collectives: 27 us -> 31 us  [step(): lax.all_gather(partner, COL_GROUP, axis=0, tiled=True, axis_index_groups=...]
    all_to_all x2, waiting for transfers between devices: 0.01 us -> 1.57 us  [exchange(): lax.all_to_all(value, axes, 0, 0, tiled=True, axis_index_groups=groups)]
    ppermute x1, starting transfers between devices: 5.6 us -> 4.03 us  [step(): received = lax.ppermute(halves[0], CORE, [(0, 1), (1, 0)])]
  transfers between devices with their start and end apart: 5 -> 5, of which waited for: 2 -> 3; matrix products, arithmetic and copies ran while one was open for 0% -> 0% of each run, Pallas kernels for 4% -> 4%
where the time goes in v4:
time: 97.1 us; the launch traced here: 95.4 us
  blocking collectives  51 us (53%)
  starting transfers between devices  26.7 us (27%)
  Pallas kernels  8.51 us (9%)
  waiting for transfers between devices  6.84 us (7%)
  local copies, waits for them, and re-layouts  1.68 us (2%)
    all_gather x1, blocking collectives, step(): lax.all_gather(partner, COL_GROUP, axis=0, tiled=True, axis_index_groups=...  31 us
    all_to_all x2, starting transfers between devices, exchange(): lax.all_to_all(value, axes, 0, 0, tiled=True, axis_index_groups=groups)  17 us
    all_to_all x1, blocking collectives, exchange(): lax.all_to_all(value, axes, 0, 0, tiled=True, axis_index_groups=groups)  12.5 us
    pallas_call x5, Pallas kernels, call(): pl.pallas_call(kernel, out_shape=outs, in_specs=[VMEM] * len(args), out_s...  8.51 us
    all_gather x1, blocking collectives, step(): lax.all_gather(jnp.stack([row_parts, far_parts]), (XH, CORE), axis=0, til...  7.48 us
    ppermute x1, waiting for transfers between devices, step(): partner = lax.ppermute(own, PAIR, [(0, 1), (1, 0)])  5 us
    ppermute x1, starting transfers between devices, step(): received = lax.ppermute(halves[0], CORE, [(0, 1), (1, 0)])  4.03 us
    ppermute x1, starting transfers between devices, step(): far_parts = lax.ppermute(row_parts, Z0, [(0, 1), (1, 0)])  3.77 us
  transfers between devices with their start and end apart: 5, of which 3 were waited for; matrix products, arithmetic and copies ran while one was open for 0% of the time, Pallas kernels for 4%

profile of v4, /device:TPU:1, one launch (start us, length us, event | category | flops | bytes accessed | tf_op | source)
XLA Modules:
  0.0 95.4 jit_solution(2727479133502012750)
XLA Ops:
  0.6 1.7 %broadcast_in_dim.11 = bf16[8,128,256]{2,1,0:T(8,128)(2,1)} broadcast(bf16[128,256]{1,0:T(8,128)(2,1)} %bitcast.10), dimensions={1,2} | broadcast | bytes 589824 | tf_op jit(solution)/shard_map/broadcast_in_dim | solution.py:153
  2.3 0.0 copy-start
  2.3 10.4 %all-to-all-start = ((bf16[8,128,256]{2,1,0:T(8,128)(2,1)}), bf16[8,128,256]{2,1,0:T(8,128)(2,1)S(1)}, u32[]{:S(2)}, u32[]{:S(2)}) async-start(bf16[8,128,256]{2,1,0:T(8,128)(2,1)} %broadcast_in_dim.11), calls=%async_computation | async-start | bytes 1048576 | tf_op jit(solution)/shard_map/all_to_all | solution.py:143
  12.7 0.0 copy-done
  12.7 1.9 %collective-permute-start = (bf16[128,256]{1,0:T(8,128)(2,1)S(1)}, bf16[128,256]{1,0:T(8,128)(2,1)S(1)}, u32[]{:S(2)}, u32[]{:S(2)}) collective-permute-start(bf16[128,256]{1,0:T(8,128)(2,1)S(1)} %bitcast.11), channel_id=1, source_target_pairs={{0,256},{256,0},{1,257},{257,1},{2,258},{258,2},{3,259},{259,3},{4... | collective-permute-start | bytes 196616 | tf_op jit(solution)/shard_map/ppermute | solution.py:152
  14.6 5.0 %collective-permute-done.partner_ref = bf16[128,256]{1,0:T(8,128)(2,1)S(1)} collective-permute-done((bf16[128,256]{1,0:T(8,128)(2,1)S(1)}, bf16[128,256]{1,0:T(8,128)(2,1)S(1)}, u32[]{:S(2)}, u32[]{:S(2)}) %collective-permute-start) | collective-permute-done | bytes 65568 | tf_op jit(solution)/shard_map/ppermute | solution.py:152
  19.6 31.0 %all_gather.9.col_ref = bf16[1024,256]{1,0:T(8,128)(2,1)S(1)} all-gather(bf16[128,256]{1,0:T(8,128)(2,1)S(1)} %collective-permute-done.partner_ref), channel_id=1, replica_groups={{0,5,8,13,16,21,24,29},{1,4,9,12,17,20,25,28},{2,7,10,15,18,23,26,31},{..., dimensions={0}, use_global_device_ids=true | all-gather | bytes 589824 | tf_op jit(solution)/shard_map/all_gather | solution.py:155
  50.5 0.0 all-to-all-done
  50.5 2.7 %shard_map.49 = (f32[8,128]{1,0:T(8,128)S(1)}, f32[8,8,128]{2,1,0:T(8,128)}) custom-call(bf16[1024,256]{1,0:T(8,128)(2,1)S(1)} %bitcast.6, bf16[1024,256]{1,0:T(8,128)(2,1)S(1)} %all_gather.9.col_ref), custom_call_target="tpu_custom_call" | custom-call | flops 1073741824 | bytes 1085440 | tf_op jit(solution)/shard_map/pallas_call | solution.py:124
  53.2 3.8 %collective-permute-start.1 = (f32[8,128]{1,0:T(8,128)S(1)}, f32[8,128]{1,0:T(8,128)S(1)}, u32[]{:S(2)}, u32[]{:S(2)}) collective-permute-start(f32[8,128]{1,0:T(8,128)S(1)} %get-tuple-element.10), channel_id=1, source_target_pairs={{0,2},{2,0},{1,3},{3,1},{4,6},{6,4},{5,7},{7,5},{8,10},{10,8},{9,1... | collective-permute-start | bytes 12296 | tf_op jit(solution)/shard_map/ppermute | solution.py:168
  57.0 6.6 %all-to-all-start.1 = ((f32[8,8,128]{2,1,0:T(8,128)}), f32[8,8,128]{2,1,0:T(8,128)S(1)}, u32[]{:S(2)}, u32[]{:S(2)}) async-start(f32[8,8,128]{2,1,0:T(8,128)} %get-tuple-element.9), calls=%async_computation.1 | async-start | bytes 65536 | tf_op jit(solution)/shard_map/all_to_all | solution.py:143
  63.6 0.0 collective-permute-done.1
  63.6 0.0 copy-start.1
  63.7 7.5 %all-gather = f32[8,8,128]{2,1,0:T(8,128)S(1)} all-gather(f32[2,8,128]{2,1,0:T(8,128)S(1)} %pad_maximum_fusion), channel_id=2, replica_groups=mesh['pair'=2,'rest'=4,'xh'=2,'zp'=8,'z0'=2,'core'=2] {'xh','core'}, dimensions={0}, use_global_device_ids=true | all-gather | bytes 40960 | tf_op jit(solution)/shard_map/all_gather | solution.py:169
  71.1 0.0 copy-done.1
  71.1 2.7 %shard_map.50 = (f32[8,128,256]{2,1,0:T(8,128)S(1)}, f32[1,128]{1,0:T(1,128)}, f32[1,128]{1,0:T(1,128)}, f32[128,256]{1,0:T(8,128)S(1)}) custom-call(bf16[1024,256]{1,0:T(8,128)(2,1)S(1)} %bitcast.7, bf16[1024,256]{1,0:T(8,128)(2,1)S(1)} %all_gather.9.col_ref, f32[4,2,8,128]{3,2,1,0:T(8,128)S(1)} %bitcast.13, bf16[128,256]{1,0:T(8,128)(2,1)S(1)} %bitcast.12, ...), custom_call_target="tpu_custom_call" | custom-call | flops 1073741824 | bytes 2397184 | tf_op jit(solution)/shard_map/pallas_call | solution.py:124
  73.8 1.6 %all-to-all-done.1.parts_ref = f32[8,8,128]{2,1,0:T(8,128)S(1)} async-done(((f32[8,8,128]{2,1,0:T(8,128)}), f32[8,8,128]{2,1,0:T(8,128)S(1)}, u32[]{:S(2)}, u32[]{:S(2)}) %all-to-all-start.1) | async-done | bytes 32800 | tf_op jit(solution)/shard_map/all_to_all | solution.py:143
  75.4 1.2 %shard_map.52 = f32[4,128,256]{2,1,0:T(8,128)S(1)} custom-call(bf16[1024,256]{1,0:T(8,128)(2,1)S(1)} %bitcast.8, bf16[1024,256]{1,0:T(8,128)(2,1)S(1)} %all_gather.9.col_ref, f32[8,8,128]{2,1,0:T(8,128)S(1)} %all-to-all-done.1.parts_ref, f32[8,128,256]{2,1,0:T(8,128)S(1)} %get-tuple-element.11.own_grad_ref), custom_call_target="tpu_custom_call" | custom-call | flops 536870912 | bytes 2654208 | tf_op jit(solution)/shard_map/pallas_call | solution.py:124
  76.6 4.0 %collective-permute-start.2 = (f32[4,128,256]{2,1,0:T(8,128)S(1)}, f32[4,128,256]{2,1,0:T(8,128)S(1)}, u32[]{:S(2)}, u32[]{:S(2)}) collective-permute-start(f32[4,128,256]{2,1,0:T(8,128)S(1)} %shard_map.52), channel_id=1, source_target_pairs={{0,1},{1,0},{2,3},{3,2},{4,5},{5,4},{6,7},{7,6},{8,9},{9,8},{10,11... | collective-permute-start | bytes 1572872 | tf_op jit(solution)/shard_map/ppermute | solution.py:192
  80.6 1.2 %shard_map.51 = f32[4,128,256]{2,1,0:T(8,128)S(1)} custom-call(bf16[1024,256]{1,0:T(8,128)(2,1)S(1)} %bitcast.9, bf16[1024,256]{1,0:T(8,128)(2,1)S(1)} %all_gather.9.col_ref, f32[8,8,128]{2,1,0:T(8,128)S(1)} %all-to-all-done.1.parts_ref, f32[8,128,256]{2,1,0:T(8,128)S(1)} %get-tuple-element.11.own_grad_ref), custom_call_target="tpu_custom_call" | custom-call | flops 536870912 | bytes 2654208 | tf_op jit(solution)/shard_map/pallas_call | solution.py:124
  81.9 0.3 collective-permute-done.2
  82.2 0.1 add.3
  82.2 12.5 %all_to_all.15.parts_ref = f32[4,128,256]{2,1,0:T(8,128)S(1)} all-to-all(f32[4,128,256]{2,1,0:T(8,128)S(1)} %add.3), channel_id=1, replica_groups=mesh['pair'=2,'rest'=4,'xh'=2,'zp'=8,'z0'=2,'core'=2] {'xh','z0'}, dimensions={0} | all-to-all | bytes 1048576 | tf_op jit(solution)/shard_map/all_to_all | solution.py:143
  94.8 0.7 shard_map.53
  (1 shorter events, 0.0 us)
Async XLA Ops:
  2.3 10.4 %copy-start = (bf16[1,128,256]{2,1,0:T(8,128)(2,1)S(1)}, bf16[1,128,256]{2,1,0:T(8,128)(2,1)}, u32[]{:S(2)}) copy-start(bf16[1,128,256]{2,1,0:T(8,128)(2,1)} %param.2) | copy-start | bytes 196612
  2.3 48.2 %all-to-all-start = ((bf16[8,128,256]{2,1,0:T(8,128)(2,1)}), bf16[8,128,256]{2,1,0:T(8,128)(2,1)S(1)}, u32[]{:S(2)}, u32[]{:S(2)}) async-start(bf16[8,128,256]{2,1,0:T(8,128)(2,1)} %broadcast_in_dim.11), calls=%async_computation | async-start | bytes 1048576 | tf_op jit(solution)/shard_map/all_to_all | solution.py:143
  12.7 6.9 %collective-permute-start = (bf16[128,256]{1,0:T(8,128)(2,1)S(1)}, bf16[128,256]{1,0:T(8,128)(2,1)S(1)}, u32[]{:S(2)}, u32[]{:S(2)}) collective-permute-start(bf16[128,256]{1,0:T(8,128)(2,1)S(1)} %bitcast.11), channel_id=1, source_target_pairs={{0,256},{256,0},{1,257},{257,1},{2,258},{258,2},{3,259},{259,3},{4... | collective-permute-start | bytes 196616 | tf_op jit(solution)/shard_map/ppermute | solution.py:152
  53.2 10.4 %collective-permute-start.1 = (f32[8,128]{1,0:T(8,128)S(1)}, f32[8,128]{1,0:T(8,128)S(1)}, u32[]{:S(2)}, u32[]{:S(2)}) collective-permute-start(f32[8,128]{1,0:T(8,128)S(1)} %get-tuple-element.10), channel_id=1, source_target_pairs={{0,2},{2,0},{1,3},{3,1},{4,6},{6,4},{5,7},{7,5},{8,10},{10,8},{9,1... | collective-permute-start | bytes 12296 | tf_op jit(solution)/shard_map/ppermute | solution.py:168
  57.0 18.3 %all-to-all-start.1 = ((f32[8,8,128]{2,1,0:T(8,128)}), f32[8,8,128]{2,1,0:T(8,128)S(1)}, u32[]{:S(2)}, u32[]{:S(2)}) async-start(f32[8,8,128]{2,1,0:T(8,128)} %get-tuple-element.9), calls=%async_computation.1 | async-start | bytes 65536 | tf_op jit(solution)/shard_map/all_to_all | solution.py:143
  63.6 7.5 %copy-start.1 = (s32[8,128]{1,0:T(8,128)S(1)}, s32[8,128]{1,0:T(8,128)}, u32[]{:S(2)}) copy-start(s32[8,128]{1,0:T(8,128)} %positive_ref.1) | copy-start | bytes 12292
  76.6 5.6 %collective-permute-start.2 = (f32[4,128,256]{2,1,0:T(8,128)S(1)}, f32[4,128,256]{2,1,0:T(8,128)S(1)}, u32[]{:S(2)}, u32[]{:S(2)}) collective-permute-start(f32[4,128,256]{2,1,0:T(8,128)S(1)} %shard_map.52), channel_id=1, source_target_pairs={{0,1},{1,0},{2,3},{3,2},{4,5},{5,4},{6,7},{7,6},{8,9},{9,8},{10,11... | collective-permute-start | bytes 1572872 | tf_op jit(solution)/shard_map/ppermute | solution.py:192

commit v5 on v4

--- a/solution.py
+++ b/solution.py
@@ -16,6 +16,7 @@
 XH, ZP, Z0, CORE = "xh", "zp", "z0", "core"
 ROW_GROUP = (XH, Z0, CORE)
 COL_GROUP = (ZP, CORE)
+BATCHED = 4
 VMEM = pl.BlockSpec(memory_space=pltpu.VMEM)
 
 
@@ -31,7 +32,7 @@
 
 
 def lse_kernel(row_ref, col_ref, row_lse_ref, col_lse_ref, score_ref):
-    step = 256
+    step = 512
     for left, right, out in ((row_ref, col_ref, col_lse_ref), (col_ref, row_ref, row_lse_ref)):
         count, width = left.shape[0], right.shape[0]
         top = jnp.full((8, width), -1e30, jnp.float32)
@@ -61,14 +62,22 @@
     totals = combine(parts_ref[...].reshape(groups * halves, tile_rows, lanes))
     totals_scratch[...] = totals
     block_rows = totals.shape[1]
-    width = col_ref.shape[0]
-    for i in range(totals.shape[0]):
-        shift = jnp.broadcast_to(totals[i : i + 1, :], (128, block_rows)).T
-        scores = score_block(row_ref[i * block_rows : (i + 1) * block_rows, :], col_ref[...])
-        weights = jnp.exp2(scores - jnp.concatenate([shift] * (width // 128), axis=1))
-        grad_ref[i] = jnp.dot(
+    tiles = col_ref.shape[0] // 128
+    for first in range(0, totals.shape[0], BATCHED):
+        shift = jnp.concatenate(
+            [
+                jnp.broadcast_to(totals[i : i + 1, :], (128, block_rows)).T
+                for i in range(first, first + BATCHED)
+            ],
+            axis=0,
+        )
+        rows = row_ref[first * block_rows : (first + BATCHED) * block_rows, :]
+        scores = score_block(rows, col_ref[...])
+        weights = jnp.exp2(scores - jnp.concatenate([shift] * tiles, axis=1))
+        part = jnp.dot(
             weights.astype(jnp.bfloat16), col_ref[...], preferred_element_type=jnp.float32
         )
+        grad_ref[first : first + BATCHED] = part.reshape(BATCHED, block_rows, part.shape[1])
     rest_count = lax.axis_size(REST)
     pair = lax.axis_index(PAIR)
     view = pair * rest_count + lax.axis_index(REST)
@@ -99,14 +108,15 @@
     block_rows = grad_ref.shape[1]
     cores = lax.axis_size(CORE)
     core = lax.rem(lax.axis_index(CORE) + flip, cores)
-    for i in range(grad_ref.shape[0]):
-        block = i * cores + core
-        start = pl.multiple_of(block * block_rows, block_rows)
-        scores = score_block(row_ref[pl.ds(start, block_rows), :], col_ref[...])
-        weights = jnp.exp2(scores - shift)
-        grad_ref[i] = own_grad_ref[block] + jnp.dot(
-            weights.astype(jnp.bfloat16), col_ref[...], preferred_element_type=jnp.float32
-        )
+    blocks = [i * cores + core for i in range(grad_ref.shape[0])]
+    rows = jnp.concatenate(
+        [row_ref[pl.ds(pl.multiple_of(k * block_rows, block_rows), block_rows), :] for k in blocks],
+        axis=0,
+    )
+    weights = jnp.exp2(score_block(rows, col_ref[...]) - shift)
+    part = jnp.dot(weights.astype(jnp.bfloat16), col_ref[...], preferred_element_type=jnp.float32)
+    for i, k in enumerate(blocks):
+        grad_ref[i] = own_grad_ref[k] + part[i * block_rows : (i + 1) * block_rows, :]
 
 
 def sum_kernel(parts_ref, base_ref, out_ref):

time: 97.1 us -> 96.6 us (level)
  Pallas kernels: 8.51 us -> 6.85 us
  waiting for transfers between devices: 6.84 us -> 7.99 us
    pallas_call x5, Pallas kernels: 8.51 us -> 6.85 us  [call(): pl.pallas_call(kernel, out_shape=outs, in_specs=[VMEM] * len(args), out_s...]
  transfers between devices with their start and end apart: 5 -> 5, of which waited for: 3 -> 3; matrix products, arithmetic and copies ran while one was open for 0% -> 0% of each run, Pallas kernels for 4% -> 3%
where the time goes in v5:
time: 96.6 us; the launch traced here: 94.9 us
  blocking collectives  51 us (53%)
  starting transfers between devices  26.7 us (28%)
  waiting for transfers between devices  7.99 us (8%)
  Pallas kernels  6.85 us (7%)
  local copies, waits for them, and re-layouts  1.68 us (2%)
    all_gather x1, blocking collectives, step(): lax.all_gather(partner, COL_GROUP, axis=0, tiled=True, axis_index_groups=...  31 us
    all_to_all x2, starting transfers between devices, exchange(): lax.all_to_all(value, axes, 0, 0, tiled=True, axis_index_groups=groups)  17 us
    all_to_all x1, blocking collectives, exchange(): lax.all_to_all(value, axes, 0, 0, tiled=True, axis_index_groups=groups)  12.5 us
    all_gather x1, blocking collectives, step(): lax.all_gather(jnp.stack([row_parts, far_parts]), (XH, CORE), axis=0, til...  7.47 us
    pallas_call x5, Pallas kernels, call(): pl.pallas_call(kernel, out_shape=outs, in_specs=[VMEM] * len(args), out_s...  6.85 us
    ppermute x1, waiting for transfers between devices, step(): partner = lax.ppermute(own, PAIR, [(0, 1), (1, 0)])  5 us
    ppermute x1, starting transfers between devices, step(): received = lax.ppermute(halves[0], CORE, [(0, 1), (1, 0)])  4.03 us
    ppermute x1, starting transfers between devices, step(): far_parts = lax.ppermute(row_parts, Z0, [(0, 1), (1, 0)])  3.77 us
  transfers between devices with their start and end apart: 5, of which 3 were waited for; matrix products, arithmetic and copies ran while one was open for 0% of the time, Pallas kernels for 3%

profile of v5, /device:TPU:1, one launch (start us, length us, event | category | flops | bytes accessed | tf_op | source)
XLA Modules:
  0.0 94.9 jit_solution(13980357110072158257)
XLA Ops:
  0.6 1.7 %broadcast_in_dim.11 = bf16[8,128,256]{2,1,0:T(8,128)(2,1)} broadcast(bf16[128,256]{1,0:T(8,128)(2,1)} %bitcast.10), dimensions={1,2} | broadcast | bytes 589824 | tf_op jit(solution)/shard_map/broadcast_in_dim | solution.py:163
  2.3 0.0 copy-start
  2.3 10.4 %all-to-all-start = ((bf16[8,128,256]{2,1,0:T(8,128)(2,1)}), bf16[8,128,256]{2,1,0:T(8,128)(2,1)S(1)}, u32[]{:S(2)}, u32[]{:S(2)}) async-start(bf16[8,128,256]{2,1,0:T(8,128)(2,1)} %broadcast_in_dim.11), calls=%async_computation | async-start | bytes 1048576 | tf_op jit(solution)/shard_map/all_to_all | solution.py:153
  12.7 0.0 copy-done
  12.7 1.9 %collective-permute-start = (bf16[128,256]{1,0:T(8,128)(2,1)S(1)}, bf16[128,256]{1,0:T(8,128)(2,1)S(1)}, u32[]{:S(2)}, u32[]{:S(2)}) collective-permute-start(bf16[128,256]{1,0:T(8,128)(2,1)S(1)} %bitcast.11), channel_id=1, source_target_pairs={{0,256},{256,0},{1,257},{257,1},{2,258},{258,2},{3,259},{259,3},{4... | collective-permute-start | bytes 196616 | tf_op jit(solution)/shard_map/ppermute | solution.py:162
  14.6 5.0 %collective-permute-done.partner_ref = bf16[128,256]{1,0:T(8,128)(2,1)S(1)} collective-permute-done((bf16[128,256]{1,0:T(8,128)(2,1)S(1)}, bf16[128,256]{1,0:T(8,128)(2,1)S(1)}, u32[]{:S(2)}, u32[]{:S(2)}) %collective-permute-start) | collective-permute-done | bytes 65568 | tf_op jit(solution)/shard_map/ppermute | solution.py:162
  19.6 31.0 %all_gather.9.col_ref = bf16[1024,256]{1,0:T(8,128)(2,1)S(1)} all-gather(bf16[128,256]{1,0:T(8,128)(2,1)S(1)} %collective-permute-done.partner_ref), channel_id=1, replica_groups={{0,5,8,13,16,21,24,29},{1,4,9,12,17,20,25,28},{2,7,10,15,18,23,26,31},{..., dimensions={0}, use_global_device_ids=true | all-gather | bytes 589824 | tf_op jit(solution)/shard_map/all_gather | solution.py:165
  50.5 0.0 all-to-all-done
  50.5 2.6 %shard_map.49 = (f32[8,128]{1,0:T(8,128)S(1)}, f32[8,8,128]{2,1,0:T(8,128)}) custom-call(bf16[1024,256]{1,0:T(8,128)(2,1)S(1)} %bitcast.6, bf16[1024,256]{1,0:T(8,128)(2,1)S(1)} %all_gather.9.col_ref), custom_call_target="tpu_custom_call" | custom-call | flops 1073741824 | bytes 1085440 | tf_op jit(solution)/shard_map/pallas_call | solution.py:134
  53.1 3.8 %collective-permute-start.1 = (f32[8,128]{1,0:T(8,128)S(1)}, f32[8,128]{1,0:T(8,128)S(1)}, u32[]{:S(2)}, u32[]{:S(2)}) collective-permute-start(f32[8,128]{1,0:T(8,128)S(1)} %get-tuple-element.10), channel_id=1, source_target_pairs={{0,2},{2,0},{1,3},{3,1},{4,6},{6,4},{5,7},{7,5},{8,10},{10,8},{9,1... | collective-permute-start | bytes 12296 | tf_op jit(solution)/shard_map/ppermute | solution.py:178
  56.9 6.6 %all-to-all-start.1 = ((f32[8,8,128]{2,1,0:T(8,128)}), f32[8,8,128]{2,1,0:T(8,128)S(1)}, u32[]{:S(2)}, u32[]{:S(2)}) async-start(f32[8,8,128]{2,1,0:T(8,128)} %get-tuple-element.9), calls=%async_computation.1 | async-start | bytes 65536 | tf_op jit(solution)/shard_map/all_to_all | solution.py:153
  63.5 0.0 collective-permute-done.1
  63.5 0.0 copy-start.1
  63.5 7.5 %all-gather = f32[8,8,128]{2,1,0:T(8,128)S(1)} all-gather(f32[2,8,128]{2,1,0:T(8,128)S(1)} %pad_maximum_fusion), channel_id=2, replica_groups=mesh['pair'=2,'rest'=4,'xh'=2,'zp'=8,'z0'=2,'core'=2] {'xh','core'}, dimensions={0}, use_global_device_ids=true | all-gather | bytes 40960 | tf_op jit(solution)/shard_map/all_gather | solution.py:179
  71.0 0.0 copy-done.1
  71.0 1.9 %shard_map.50 = (f32[8,128,256]{2,1,0:T(8,128)S(1)}, f32[1,128]{1,0:T(1,128)}, f32[1,128]{1,0:T(1,128)}, f32[128,256]{1,0:T(8,128)S(1)}) custom-call(bf16[1024,256]{1,0:T(8,128)(2,1)S(1)} %bitcast.7, bf16[1024,256]{1,0:T(8,128)(2,1)S(1)} %all_gather.9.col_ref, f32[4,2,8,128]{3,2,1,0:T(8,128)S(1)} %bitcast.13, bf16[128,256]{1,0:T(8,128)(2,1)S(1)} %bitcast.12, ...), custom_call_target="tpu_custom_call" | custom-call | flops 1073741824 | bytes 2397184 | tf_op jit(solution)/shard_map/pallas_call | solution.py:134
  72.9 2.3 %all-to-all-done.1.parts_ref = f32[8,8,128]{2,1,0:T(8,128)S(1)} async-done(((f32[8,8,128]{2,1,0:T(8,128)}), f32[8,8,128]{2,1,0:T(8,128)S(1)}, u32[]{:S(2)}, u32[]{:S(2)}) %all-to-all-start.1) | async-done | bytes 32800 | tf_op jit(solution)/shard_map/all_to_all | solution.py:153
  75.2 0.9 shard_map.52
  76.1 4.0 %collective-permute-start.2 = (f32[4,128,256]{2,1,0:T(8,128)S(1)}, f32[4,128,256]{2,1,0:T(8,128)S(1)}, u32[]{:S(2)}, u32[]{:S(2)}) collective-permute-start(f32[4,128,256]{2,1,0:T(8,128)S(1)} %shard_map.52), channel_id=1, source_target_pairs={{0,1},{1,0},{2,3},{3,2},{4,5},{5,4},{6,7},{7,6},{8,9},{9,8},{10,11... | collective-permute-start | bytes 1572872 | tf_op jit(solution)/shard_map/ppermute | solution.py:202
  80.1 0.9 shard_map.51
  81.0 0.7 collective-permute-done.2
  81.6 0.1 add.3
  81.7 12.5 %all_to_all.15.parts_ref = f32[4,128,256]{2,1,0:T(8,128)S(1)} all-to-all(f32[4,128,256]{2,1,0:T(8,128)S(1)} %add.3), channel_id=1, replica_groups=mesh['pair'=2,'rest'=4,'xh'=2,'zp'=8,'z0'=2,'core'=2] {'xh','z0'}, dimensions={0} | all-to-all | bytes 1048576 | tf_op jit(solution)/shard_map/all_to_all | solution.py:153
  94.2 0.7 shard_map.53
  (1 shorter events, 0.0 us)
Async XLA Ops:
  2.3 10.4 %copy-start = (bf16[1,128,256]{2,1,0:T(8,128)(2,1)S(1)}, bf16[1,128,256]{2,1,0:T(8,128)(2,1)}, u32[]{:S(2)}) copy-start(bf16[1,128,256]{2,1,0:T(8,128)(2,1)} %param.2) | copy-start | bytes 196612
  2.3 48.2 %all-to-all-start = ((bf16[8,128,256]{2,1,0:T(8,128)(2,1)}), bf16[8,128,256]{2,1,0:T(8,128)(2,1)S(1)}, u32[]{:S(2)}, u32[]{:S(2)}) async-start(bf16[8,128,256]{2,1,0:T(8,128)(2,1)} %broadcast_in_dim.11), calls=%async_computation | async-start | bytes 1048576 | tf_op jit(solution)/shard_map/all_to_all | solution.py:153
  12.7 6.9 %collective-permute-start = (bf16[128,256]{1,0:T(8,128)(2,1)S(1)}, bf16[128,256]{1,0:T(8,128)(2,1)S(1)}, u32[]{:S(2)}, u32[]{:S(2)}) collective-permute-start(bf16[128,256]{1,0:T(8,128)(2,1)S(1)} %bitcast.11), channel_id=1, source_target_pairs={{0,256},{256,0},{1,257},{257,1},{2,258},{258,2},{3,259},{259,3},{4... | collective-permute-start | bytes 196616 | tf_op jit(solution)/shard_map/ppermute | solution.py:162
  53.1 10.4 %collective-permute-start.1 = (f32[8,128]{1,0:T(8,128)S(1)}, f32[8,128]{1,0:T(8,128)S(1)}, u32[]{:S(2)}, u32[]{:S(2)}) collective-permute-start(f32[8,128]{1,0:T(8,128)S(1)} %get-tuple-element.10), channel_id=1, source_target_pairs={{0,2},{2,0},{1,3},{3,1},{4,6},{6,4},{5,7},{7,5},{8,10},{10,8},{9,1... | collective-permute-start | bytes 12296 | tf_op jit(solution)/shard_map/ppermute | solution.py:178
  56.9 18.3 %all-to-all-start.1 = ((f32[8,8,128]{2,1,0:T(8,128)}), f32[8,8,128]{2,1,0:T(8,128)S(1)}, u32[]{:S(2)}, u32[]{:S(2)}) async-start(f32[8,8,128]{2,1,0:T(8,128)} %get-tuple-element.9), calls=%async_computation.1 | async-start | bytes 65536 | tf_op jit(solution)/shard_map/all_to_all | solution.py:153
  63.5 7.5 %copy-start.1 = (s32[8,128]{1,0:T(8,128)S(1)}, s32[8,128]{1,0:T(8,128)}, u32[]{:S(2)}) copy-start(s32[8,128]{1,0:T(8,128)} %positive_ref.1) | copy-start | bytes 12292
  76.1 5.5 %collective-permute-start.2 = (f32[4,128,256]{2,1,0:T(8,128)S(1)}, f32[4,128,256]{2,1,0:T(8,128)S(1)}, u32[]{:S(2)}, u32[]{:S(2)}) collective-permute-start(f32[4,128,256]{2,1,0:T(8,128)S(1)} %shard_map.52), channel_id=1, source_target_pairs={{0,1},{1,0},{2,3},{3,2},{4,5},{5,4},{6,7},{7,6},{8,9},{9,8},{10,11... | collective-permute-start | bytes 1572872 | tf_op jit(solution)/shard_map/ppermute | solution.py:202

commit v6 on v2

v6 whole, which is shorter than its diff:
```python
import jax
import jax.numpy as jnp
from jax import lax
from jax.experimental import pallas as pl
from jax.experimental.pallas import tpu as pltpu
from jax.sharding import Mesh, PartitionSpec as P


logit_scale = 10.0
log2_e = 1.4426950408889634
ln_2 = 0.6931471805599453

PAIR, REST = "pair", "rest"
XH, ZP, Z0, CORE = "xh", "zp", "z0", "core"
ROW_GROUP = (XH, Z0)
COL_GROUP = (ZP, CORE)
FLIP = [(0, 1), (1, 0)]
VMEM = pl.BlockSpec(memory_space=pltpu.VMEM)


def score_block(rows, cols):
    return lax.dot_general(
        rows, cols, (((1,), (1,)), ((), ())), preferred_element_type=jnp.float32
    ) * (logit_scale * log2_e)


def combine(parts):
    top = jnp.max(parts, axis=0)
    return top + jnp.log(jnp.sum(jnp.exp2(parts - top[None]), axis=0)) * log2_e


def column_group():
    return lax.rem(lax.axis_index(ZP) + lax.axis_index(CORE), lax.axis_size(CORE))


def to_tile(row):
    return jnp.concatenate([row[:, i : i + 128] for i in range(0, row.shape[1], 128)], axis=0)


def lse_over_left(left, right, score_ref):
    count, width = left.shape[0], right.shape[0]
    step = 512
    top = jnp.full((8, width), -1e30, jnp.float32)
    for start in range(0, count, step):
        block = score_block(left[start : start + step, :], right[...])
        score_ref[start : start + step, :width] = block
        top = jnp.maximum(top, jnp.max(block.reshape(step // 8, 8, width), axis=0))
    top = jnp.max(top, axis=0, keepdims=True)
    total = jnp.zeros((8, width), jnp.float32)
    for start in range(0, count, step):
        block = jnp.exp2(score_ref[start : start + step, :width] - top)
        total = total + jnp.sum(block.reshape(step // 8, 8, width), axis=0)
    return top + jnp.log(jnp.sum(total, axis=0, keepdims=True)) * log2_e


def near_lse_kernel(row_ref, col_ref, row_lse_ref, col_lse_ref, score_ref):
    col_lse_ref[...] = to_tile(lse_over_left(row_ref, col_ref, score_ref))
    row_lse_ref[...] = to_tile(lse_over_left(col_ref, row_ref, score_ref))


def far_lse_kernel(row_ref, col_ref, near_row_ref, near_col_ref, row_lse_ref, col_lse_ref, score_ref):
    far = to_tile(lse_over_left(row_ref, col_ref, score_ref))
    row_lse_ref[0] = near_row_ref[...]
    row_lse_ref[1] = to_tile(lse_over_left(col_ref, row_ref, score_ref))
    tile_rows = far.shape[0]
    group = column_group()
    near = near_col_ref[...]
    first = jnp.where(group == 0, near, far)
    second = jnp.where(group == 0, far, near)
    for peer in range(col_lse_ref.shape[0]):
        col_lse_ref[peer, :tile_rows, :] = first
        col_lse_ref[peer, tile_rows:, :] = second


def own_kernel(
    row_ref, near_ref, far_ref, parts_ref, own_ref, partner_ref, positive_ref,
    grad_ref, totals_ref, loss_ref, base_ref, totals_scratch,
):
    groups, halves, blocks, block_rows = parts_ref.shape
    totals = combine(parts_ref[...].reshape(groups * halves, blocks, block_rows))
    totals_scratch[:blocks, :] = totals
    shift = jnp.concatenate(
        [
            jnp.broadcast_to(totals[i : i + 1, :], (128, block_rows)).T for i in range(blocks)
        ],
        axis=0,
    )
    shift = jnp.concatenate([shift] * (near_ref.shape[0] // 128), axis=1)
    part = None
    for cols in (near_ref, far_ref):
        weights = jnp.exp2(score_block(row_ref[...], cols[...]) - shift)
        more = jnp.dot(
            weights.astype(jnp.bfloat16), cols[...], preferred_element_type=jnp.float32
        )
        part = more if part is None else part + more
    grad_ref[...] = part.reshape(grad_ref.shape)
    rest_count = lax.axis_size(REST)
    pair = lax.axis_index(PAIR)
    view = pair * rest_count + lax.axis_index(REST)
    far = (1 - pair) * rest_count + lax.axis_index(REST)
    own_match = positive_ref[pl.ds(view, 1), :]
    far_match = positive_ref[pl.ds(far, 1), :]
    row_ids = lax.broadcasted_iota(jnp.int32, (block_rows, block_rows), 0)
    own_hot = (row_ids == own_match).astype(jnp.float32).astype(jnp.bfloat16)
    far_hot = (row_ids == far_match).astype(jnp.float32).astype(jnp.bfloat16)
    partner = partner_ref[...]
    pos_rows = lax.dot_general(
        own_hot, partner, (((0,), (0,)), ((), ())), preferred_element_type=jnp.float32
    )
    matched = jnp.dot(far_hot, partner, preferred_element_type=jnp.float32)
    base_ref[...] = (pos_rows + matched) * -logit_scale
    product = own_ref[...].astype(jnp.float32) * pos_rows
    pos_score = jnp.sum(product.T, axis=0, keepdims=True) * logit_scale
    place = lax.axis_index(XH) * lax.axis_size(Z0) + lax.axis_index(Z0)
    own_totals = totals_scratch[pl.ds(place, 1), :] * ln_2
    totals_ref[...] = own_totals
    loss_ref[...] = own_totals - pos_score


def side_kernel(row_ref, near_ref, far_ref, parts_ref, own_grad_ref, grad_ref):
    totals = combine(parts_ref[...])
    half = totals.shape[0] // 2
    group = column_group()
    part = own_grad_ref[...].reshape(row_ref.shape[0], -1)
    for cols, flip in ((near_ref, 0), (far_ref, 1)):
        mine = jnp.where(jnp.bitwise_xor(group, flip) == 0, totals[:half, :], totals[half:, :])
        shift = jnp.concatenate([mine[i : i + 1, :] for i in range(half)], axis=1)
        weights = jnp.exp2(score_block(row_ref[...], cols[...]) - shift)
        part = part + jnp.dot(
            weights.astype(jnp.bfloat16), cols[...], preferred_element_type=jnp.float32
        )
    grad_ref[...] = part.reshape(grad_ref.shape)


def sum_kernel(parts_ref, base_ref, out_ref):
    total = parts_ref[0]
    for i in range(1, parts_ref.shape[0]):
        total = total + parts_ref[i]
    out_ref[...] = total * logit_scale + base_ref[...]


def call(kernel, outs, *args, flops=0, transcendentals=0, scratch=()):
    single = not isinstance(outs, tuple)
    out_list = (outs,) if single else outs
    moved = sum(a.size * a.dtype.itemsize for a in args)
    moved += sum(o.size * o.dtype.itemsize for o in out_list)
    return pl.pallas_call(
        kernel,
        out_shape=outs,
        in_specs=[VMEM] * len(args),
        out_specs=VMEM if single else tuple([VMEM] * len(out_list)),
        scratch_shapes=list(scratch),
        compiler_params=pltpu.CompilerParams(vmem_limit_bytes=16 << 20),
        cost_estimate=pl.CostEstimate(
            flops=flops, bytes_accessed=moved, transcendentals=transcendentals
        ),
    )(*args)


def col_groups():
    planes, cores = lax.axis_size(ZP), lax.axis_size(CORE)
    return [[p * cores + (p + g) % cores for p in range(planes)] for g in range(cores)]


def exchange(value, axes, groups=None):
    return lax.all_to_all(value, axes, 0, 0, tiled=True, axis_index_groups=groups)


def step(embeddings, positive):
    own = embeddings[0]
    row_count, width = own.shape
    rows_n = lax.axis_size(XH) * lax.axis_size(Z0)
    cols_n = lax.axis_size(ZP) * lax.axis_size(CORE)
    f32, shape = jnp.float32, jax.ShapeDtypeStruct
    partner = lax.ppermute(own, PAIR, FLIP)
    rows = exchange(jnp.broadcast_to(own[None], (rows_n, row_count, width)), ROW_GROUP)
    rows = rows.reshape(rows_n * row_count, width)
    near = lax.all_gather(partner, COL_GROUP, axis=0, tiled=True, axis_index_groups=col_groups())
    far = lax.ppermute(near, CORE, FLIP)
    row_tiles, col_tiles = rows.shape[0] // 128, near.shape[0] // 128
    area = rows.shape[0] * near.shape[0]
    scratch = [pltpu.VMEM((max(rows.shape[0], near.shape[0]),) * 2, f32)]
    near_row, near_col = call(
        near_lse_kernel,
        (shape((row_tiles, 128), f32), shape((col_tiles, 128), f32)),
        rows, near,
        flops=4 * area * width, transcendentals=2 * area, scratch=scratch,
    )
    row_parts, col_parts = call(
        far_lse_kernel,
        (shape((2, row_tiles, 128), f32), shape((cols_n, 2 * col_tiles, 128), f32)),
        rows, far, near_row, near_col,
        flops=4 * area * width, transcendentals=2 * area, scratch=scratch,
    )
    row_parts = lax.all_gather(row_parts, ROW_GROUP, axis=0, tiled=False)
    col_parts = exchange(col_parts, COL_GROUP)
    grads, totals, row_loss, base = call(
        own_kernel,
        (
            shape((rows_n, row_count, width), f32),
            shape((1, row_count), f32),
            shape((1, row_count), f32),
            shape((row_count, width), f32),
        ),
        rows, near, far, row_parts, own, partner, positive,
        flops=8 * area * width, transcendentals=2 * area,
        scratch=[pltpu.VMEM((8, 128), f32)],
    )
    grads = call(
        side_kernel,
        shape((rows_n, row_count, width), f32),
        rows, near, far, col_parts, grads,
        flops=8 * area * width, transcendentals=2 * area,
    )
    grads = exchange(grads, ROW_GROUP)
    gradients = call(sum_kernel, shape((row_count, width), f32), grads, base)
    return (gradients[None], totals, row_loss)


def solution(mesh):
    view, batch = mesh.shape["view"], mesh.shape["batch"]
    inner = Mesh(
        mesh.devices.reshape(2, view // 2, 2, batch // 8, 2, 2), (PAIR, REST, XH, ZP, Z0, CORE)
    )
    v, b = (PAIR, REST), (XH, ZP, Z0, CORE)
    return jax.shard_map(
        step,
        mesh=inner,
        in_specs=(P(v, b, None), P(None, b)),
        out_specs=(P(v, b, None), P(v, b), P(v, b)),
        check_vma=False,
    )
```

time: 107 us -> 95.6 us (0.89)
  the two profiles are of different devices: /device:TPU:1 before, /device:TPU:24 now
where the time goes in v6:
time: 95.6 us; the launch traced here: 95.2 us
  blocking collectives  61.9 us (65%)
  starting transfers between devices  18.6 us (19%)
  Pallas kernels  7.35 us (8%)
  waiting for transfers between devices  5.01 us (5%)
  local copies, waits for them, and re-layouts  1.58 us (2%)
    all_gather x1, blocking collectives, step(): lax.all_gather(partner, COL_GROUP, axis=0, tiled=True, axis_index_groups=...  32.5 us
    all_gather x1, blocking collectives, step(): row_parts = lax.all_gather(row_parts, ROW_GROUP, axis=0, tiled=False)  16.8 us
    all_to_all x2, starting transfers between devices, exchange(): lax.all_to_all(value, axes, 0, 0, tiled=True, axis_index_groups=groups)  13.6 us
    all_to_all x1, blocking collectives, exchange(): lax.all_to_all(value, axes, 0, 0, tiled=True, axis_index_groups=groups)  12.6 us
    pallas_call x5, Pallas kernels, call(): pl.pallas_call(kernel, out_shape=outs, in_specs=[VMEM] * len(args), out_s...  7.35 us
    ppermute x1, waiting for transfers between devices, step(): partner = lax.ppermute(own, PAIR, FLIP)  4.51 us
    ppermute x1, starting transfers between devices, step(): partner = lax.ppermute(own, PAIR, FLIP)  3.13 us
  transfers between devices with their start and end apart: 4, of which 2 were waited for; matrix products, arithmetic and copies ran while one was open for 0% of the time, Pallas kernels for 4%

profile of v6, /device:TPU:24, one launch (start us, length us, event | category | flops | bytes accessed | tf_op | source)
XLA Modules:
  0.0 95.2 jit_solution(2332117588445447193)
XLA Ops:
  0.6 1.6 %broadcast_in_dim.11 = bf16[4,128,256]{2,1,0:T(8,128)(2,1)} broadcast(bf16[128,256]{1,0:T(8,128)(2,1)} %bitcast.8), dimensions={1,2} | broadcast | bytes 327680 | tf_op jit(solution)/shard_map/broadcast_in_dim | solution.py:176
  2.2 0.0 copy-start
  2.2 5.8 %all-to-all-start = ((bf16[4,128,256]{2,1,0:T(8,128)(2,1)}), bf16[4,128,256]{2,1,0:T(8,128)(2,1)S(1)}, u32[]{:S(2)}, u32[]{:S(2)}) async-start(bf16[4,128,256]{2,1,0:T(8,128)(2,1)} %broadcast_in_dim.11), calls=%async_computation | async-start | bytes 524288 | tf_op jit(solution)/shard_map/all_to_all | solution.py:166
  8.0 0.0 copy-done
  8.0 3.1 %collective-permute-start = (bf16[128,256]{1,0:T(8,128)(2,1)S(1)}, bf16[128,256]{1,0:T(8,128)(2,1)S(1)}, u32[]{:S(2)}, u32[]{:S(2)}) collective-permute-start(bf16[128,256]{1,0:T(8,128)(2,1)S(1)} %bitcast.9), channel_id=1, source_target_pairs={{0,256},{256,0},{1,257},{257,1},{2,258},{258,2},{3,259},{259,3},{4... | collective-permute-start | bytes 196616 | tf_op jit(solution)/shard_map/ppermute | solution.py:175
  11.1 4.5 %collective-permute-done.partner_ref = bf16[128,256]{1,0:T(8,128)(2,1)S(1)} collective-permute-done((bf16[128,256]{1,0:T(8,128)(2,1)S(1)}, bf16[128,256]{1,0:T(8,128)(2,1)S(1)}, u32[]{:S(2)}, u32[]{:S(2)}) %collective-permute-start) | collective-permute-done | bytes 65568 | tf_op jit(solution)/shard_map/ppermute | solution.py:175
  15.6 32.5 %all_gather.9.col_ref.near_ref = bf16[1024,256]{1,0:T(8,128)(2,1)S(1)} all-gather(bf16[128,256]{1,0:T(8,128)(2,1)S(1)} %collective-permute-done.partner_ref), channel_id=1, replica_groups={{0,5,8,13,16,21,24,29},{1,4,9,12,17,20,25,28},{2,7,10,15,18,23,26,31},{..., dimensions={0}, use_global_device_ids=true | all-gather | bytes 589824 | tf_op jit(solution)/shard_map/all_gather | solution.py:178
  48.1 1.9 %collective-permute-start.1 = (bf16[1024,256]{1,0:T(8,128)(2,1)S(1)}, bf16[1024,256]{1,0:T(8,128)(2,1)S(1)}, u32[]{:S(2)}, u32[]{:S(2)}) collective-permute-start(bf16[1024,256]{1,0:T(8,128)(2,1)S(1)} %all_gather.9.col_ref.near_ref), channel_id=1, source_target_pairs={{0,1},{1,0},{2,3},{3,2},{4,5},{5,4},{6,7},{7,6},{8,9},{9,8},{10,11... | collective-permute-start | bytes 1572872 | tf_op jit(solution)/shard_map/ppermute | solution.py:179
  50.1 0.0 all-to-all-done
  50.1 1.4 %shard_map.49 = (f32[4,128]{1,0:T(4,128)S(1)}, f32[8,128]{1,0:T(8,128)S(1)}) custom-call(bf16[512,256]{1,0:T(8,128)(2,1)S(1)} %bitcast.4, bf16[1024,256]{1,0:T(8,128)(2,1)S(1)} %all_gather.9.col_ref.near_ref), custom_call_target="tpu_custom_call" | custom-call | flops 536870912 | bytes 792576 | tf_op jit(solution)/shard_map/pallas_call | solution.py:147
  51.4 0.5 collective-permute-done.1.col_ref.far_ref
  51.9 1.5 %shard_map.50 = (f32[2,4,128]{2,1,0:T(4,128)S(1)}, f32[16,16,128]{2,1,0:T(8,128)}) custom-call(bf16[512,256]{1,0:T(8,128)(2,1)S(1)} %bitcast.5, bf16[1024,256]{1,0:T(8,128)(2,1)S(1)} %collective-permute-done.1.col_ref.far_ref, f32[4,128]{1,0:T(4,128)S(1)} %get-tuple-element.11.near_row_ref, f32[8,128]{1,0:T(8,128)S(1)} %get-tuple-element.12.near_col_ref), custom_call_target="tpu_custom_call" | custom-call | flops 536870912 | bytes 927744 | tf_op jit(solution)/shard_map/pallas_call | solution.py:147
  53.5 7.8 %all-to-all-start.1 = ((f32[16,16,128]{2,1,0:T(8,128)}), f32[16,16,128]{2,1,0:T(8,128)S(1)}, u32[]{:S(2)}, u32[]{:S(2)}) async-start(f32[16,16,128]{2,1,0:T(8,128)} %get-tuple-element.13), calls=%async_computation.1 | async-start | bytes 262144 | tf_op jit(solution)/shard_map/all_to_all | solution.py:166
  61.3 0.0 copy-start.1
  61.3 16.8 %all-gather = f32[8,4,128]{2,1,0:T(4,128)S(1)} all-gather(f32[2,4,128]{2,1,0:T(4,128)S(1)} %get-tuple-element.14), channel_id=2, replica_groups=mesh['pair'=2,'rest'=4,'xh'=2,'zp'=8,'z0'=2,'core'=2] {'xh','z0'}, dimensions={0}, use_global_device_ids=true | all-gather | bytes 20480 | tf_op jit(solution)/shard_map/all_gather | solution.py:195
  78.1 0.0 copy-done.1
  78.1 2.4 %shard_map.51 = (f32[4,128,256]{2,1,0:T(8,128)S(1)}, f32[1,128]{1,0:T(1,128)}, f32[1,128]{1,0:T(1,128)}, f32[128,256]{1,0:T(8,128)S(1)}) custom-call(bf16[512,256]{1,0:T(8,128)(2,1)S(1)} %bitcast.6, bf16[1024,256]{1,0:T(8,128)(2,1)S(1)} %all_gather.9.col_ref.near_ref, bf16[1024,256]{1,0:T(8,128)(2,1)S(1)} %collective-permute-done.1.col_ref.far_ref, ...), custom_call_target="tpu_custom_call" | custom-call | flops 1073741824 | bytes 2118656 | tf_op jit(solution)/shard_map/pallas_call | solution.py:147
  80.5 0.0 all-to-all-done.1.parts_ref
  80.5 1.4 %shard_map.52 = f32[4,128,256]{2,1,0:T(8,128)S(1)} custom-call(bf16[512,256]{1,0:T(8,128)(2,1)S(1)} %bitcast.7, bf16[1024,256]{1,0:T(8,128)(2,1)S(1)} %all_gather.9.col_ref.near_ref, bf16[1024,256]{1,0:T(8,128)(2,1)S(1)} %collective-permute-done.1.col_ref.far_ref, f32[16,16,128]{2,1,0:T(8,128)S(1)} %all-to-all-done.1.parts_ref, ...), custom_call_target="tpu_custom_call" | custom-call | flops 1073741824 | bytes 2490368 | tf_op jit(solution)/shard_map/pallas_call | solution.py:147
  81.9 12.6 %all_to_all.15.parts_ref = f32[4,128,256]{2,1,0:T(8,128)S(1)} all-to-all(f32[4,128,256]{2,1,0:T(8,128)S(1)} %shard_map.52), channel_id=1, replica_groups=mesh['pair'=2,'rest'=4,'xh'=2,'zp'=8,'z0'=2,'core'=2] {'xh','z0'}, dimensions={0} | all-to-all | bytes 1048576 | tf_op jit(solution)/shard_map/all_to_all | solution.py:166
  94.5 0.7 shard_map.53
Async XLA Ops:
  2.2 5.8 %copy-start = (bf16[1,128,256]{2,1,0:T(8,128)(2,1)S(1)}, bf16[1,128,256]{2,1,0:T(8,128)(2,1)}, u32[]{:S(2)}) copy-start(bf16[1,128,256]{2,1,0:T(8,128)(2,1)} %param.2) | copy-start | bytes 196612
  2.2 47.9 %all-to-all-start = ((bf16[4,128,256]{2,1,0:T(8,128)(2,1)}), bf16[4,128,256]{2,1,0:T(8,128)(2,1)S(1)}, u32[]{:S(2)}, u32[]{:S(2)}) async-start(bf16[4,128,256]{2,1,0:T(8,128)(2,1)} %broadcast_in_dim.11), calls=%async_computation | async-start | bytes 524288 | tf_op jit(solution)/shard_map/all_to_all | solution.py:166
  8.0 7.7 %collective-permute-start = (bf16[128,256]{1,0:T(8,128)(2,1)S(1)}, bf16[128,256]{1,0:T(8,128)(2,1)S(1)}, u32[]{:S(2)}, u32[]{:S(2)}) collective-permute-start(bf16[128,256]{1,0:T(8,128)(2,1)S(1)} %bitcast.9), channel_id=1, source_target_pairs={{0,256},{256,0},{1,257},{257,1},{2,258},{258,2},{3,259},{259,3},{4... | collective-permute-start | bytes 196616 | tf_op jit(solution)/shard_map/ppermute | solution.py:175
  48.1 3.8 %collective-permute-start.1 = (bf16[1024,256]{1,0:T(8,128)(2,1)S(1)}, bf16[1024,256]{1,0:T(8,128)(2,1)S(1)}, u32[]{:S(2)}, u32[]{:S(2)}) collective-permute-start(bf16[1024,256]{1,0:T(8,128)(2,1)S(1)} %all_gather.9.col_ref.near_ref), channel_id=1, source_target_pairs={{0,1},{1,0},{2,3},{3,2},{4,5},{5,4},{6,7},{7,6},{8,9},{9,8},{10,11... | collective-permute-start | bytes 1572872 | tf_op jit(solution)/shard_map/ppermute | solution.py:179
  53.5 27.0 %all-to-all-start.1 = ((f32[16,16,128]{2,1,0:T(8,128)}), f32[16,16,128]{2,1,0:T(8,128)S(1)}, u32[]{:S(2)}, u32[]{:S(2)}) async-start(f32[16,16,128]{2,1,0:T(8,128)} %get-tuple-element.13), calls=%async_computation.1 | async-start | bytes 262144 | tf_op jit(solution)/shard_map/all_to_all | solution.py:166
  61.3 16.8 %copy-start.1 = (s32[8,128]{1,0:T(8,128)S(1)}, s32[8,128]{1,0:T(8,128)}, u32[]{:S(2)}) copy-start(s32[8,128]{1,0:T(8,128)} %positive_ref.1) | copy-start | bytes 12292

commit v7 on v6

--- a/solution.py
+++ b/solution.py
@@ -1,3 +1,5 @@
+import functools
+
 import jax
 import jax.numpy as jnp
 from jax import lax
@@ -117,25 +119,31 @@
     loss_ref[...] = own_totals - pos_score
 
 
-def side_kernel(row_ref, near_ref, far_ref, parts_ref, own_grad_ref, grad_ref):
+def side_kernel(picks, row_ref, near_ref, far_ref, parts_ref, own_grad_ref, *grad_refs):
     totals = combine(parts_ref[...])
     half = totals.shape[0] // 2
     group = column_group()
-    part = own_grad_ref[...].reshape(row_ref.shape[0], -1)
+    block_rows = own_grad_ref.shape[1]
+    here = lax.axis_index(XH) * lax.axis_size(Z0) + lax.axis_index(Z0)
+    blocks = [jnp.bitwise_xor(here, i) for i in picks]
+    rows = jnp.concatenate(
+        [row_ref[pl.ds(pl.multiple_of(k * block_rows, block_rows), block_rows), :] for k in blocks],
+        axis=0,
+    )
+    part = jnp.concatenate([own_grad_ref[k] for k in blocks], axis=0)
     for cols, flip in ((near_ref, 0), (far_ref, 1)):
         mine = jnp.where(jnp.bitwise_xor(group, flip) == 0, totals[:half, :], totals[half:, :])
         shift = jnp.concatenate([mine[i : i + 1, :] for i in range(half)], axis=1)
-        weights = jnp.exp2(score_block(row_ref[...], cols[...]) - shift)
+        weights = jnp.exp2(score_block(rows, cols[...]) - shift)
         part = part + jnp.dot(
             weights.astype(jnp.bfloat16), cols[...], preferred_element_type=jnp.float32
         )
-    grad_ref[...] = part.reshape(grad_ref.shape)
-
-
-def sum_kernel(parts_ref, base_ref, out_ref):
-    total = parts_ref[0]
-    for i in range(1, parts_ref.shape[0]):
-        total = total + parts_ref[i]
+    for i, out in enumerate(grad_refs):
+        out[...] = part[i * block_rows : (i + 1) * block_rows, :]
+
+
+def sum_kernel(own_ref, z0_ref, xh_ref, both_ref, base_ref, out_ref):
+    total = (own_ref[...] + z0_ref[...]) + (xh_ref[...] + both_ref[...])
     out_ref[...] = total * logit_scale + base_ref[...]
 
 
@@ -206,14 +214,23 @@
         flops=8 * area * width, transcendentals=2 * area,
         scratch=[pltpu.VMEM((8, 128), f32)],
     )
-    grads = call(
-        side_kernel,
-        shape((rows_n, row_count, width), f32),
-        rows, near, far, col_parts, grads,
-        flops=8 * area * width, transcendentals=2 * area,
-    )
-    grads = exchange(grads, ROW_GROUP)
-    gradients = call(sum_kernel, shape((row_count, width), f32), grads, base)
+
+    def side(picks):
+        return call(
+            functools.partial(side_kernel, picks),
+            (shape((row_count, width), f32), shape((row_count, width), f32)),
+            rows, near, far, col_parts, grads,
+            flops=4 * area * width, transcendentals=area,
+        )
+
+    both, across = side((3, 2))
+    both = lax.ppermute(both, (XH, Z0), [(0, 3), (1, 2), (2, 1), (3, 0)])
+    across = lax.ppermute(across, XH, FLIP)
+    beside, kept = side((1, 0))
+    beside = lax.ppermute(beside, Z0, FLIP)
+    gradients = call(
+        sum_kernel, shape((row_count, width), f32), kept, beside, across, both, base
+    )
     return (gradients[None], totals, row_loss)
 
 

time: 95.6 us -> 98.2 us (1.027)
  the two profiles are of different devices: /device:TPU:24 before, /device:TPU:152 now
where the time goes in v7:
time: 98.2 us; the launch traced here: 97.7 us
  blocking collectives  45.6 us (46%)
  starting transfers between devices  32.2 us (33%)
  waiting for transfers between devices  9.93 us (10%)
  Pallas kernels  7.66 us (8%)
  local copies, waits for them, and re-layouts  1.56 us (2%)
    all_gather x1, blocking collectives, step(): lax.all_gather(partner, COL_GROUP, axis=0, tiled=True, axis_index_groups=...  28.9 us
    all_gather x1, blocking collectives, step(): row_parts = lax.all_gather(row_parts, ROW_GROUP, axis=0, tiled=False)  16.7 us
    all_to_all x2, starting transfers between devices, exchange(): lax.all_to_all(value, axes, 0, 0, tiled=True, axis_index_groups=groups)  15.9 us
    pallas_call x6, Pallas kernels, call(): pl.pallas_call(kernel, out_shape=outs, in_specs=[VMEM] * len(args), out_s...  7.66 us
    ppermute x1, starting transfers between devices, step(): both = lax.ppermute(both, (XH, Z0), [(0, 3), (1, 2), (2, 1), (3, 0)])  5.88 us
    ppermute x1, waiting for transfers between devices, step(): partner = lax.ppermute(own, PAIR, FLIP)  4.51 us
    ppermute x1, waiting for transfers between devices, step(): beside = lax.ppermute(beside, Z0, FLIP)  3.83 us
    ppermute x1, starting transfers between devices, step(): across = lax.ppermute(across, XH, FLIP)  3.51 us
  transfers between devices with their start and end apart: 7, of which 4 were waited for; matrix products, arithmetic and copies ran while one was open for 0% of the time, Pallas kernels for 5%

profile of v7, /device:TPU:152, one launch (start us, length us, event | category | flops | bytes accessed | tf_op | source)
XLA Modules:
  0.0 97.7 jit_solution(11307976691439797764)
XLA Ops:
  0.6 1.6 %broadcast_in_dim.11 = bf16[4,128,256]{2,1,0:T(8,128)(2,1)} broadcast(bf16[128,256]{1,0:T(8,128)(2,1)} %bitcast.9), dimensions={1,2} | broadcast | bytes 327680 | tf_op jit(solution)/shard_map/broadcast_in_dim | solution.py:184
  2.2 0.0 copy-start
  2.2 5.8 %all-to-all-start = ((bf16[4,128,256]{2,1,0:T(8,128)(2,1)}), bf16[4,128,256]{2,1,0:T(8,128)(2,1)S(1)}, u32[]{:S(2)}, u32[]{:S(2)}) async-start(bf16[4,128,256]{2,1,0:T(8,128)(2,1)} %broadcast_in_dim.11), calls=%async_computation | async-start | bytes 524288 | tf_op jit(solution)/shard_map/all_to_all | solution.py:174
  8.0 0.0 copy-done
  8.0 3.1 %collective-permute-start = (bf16[128,256]{1,0:T(8,128)(2,1)S(1)}, bf16[128,256]{1,0:T(8,128)(2,1)S(1)}, u32[]{:S(2)}, u32[]{:S(2)}) collective-permute-start(bf16[128,256]{1,0:T(8,128)(2,1)S(1)} %bitcast.10), channel_id=1, source_target_pairs={{0,256},{256,0},{1,257},{257,1},{2,258},{258,2},{3,259},{259,3},{4... | collective-permute-start | bytes 196616 | tf_op jit(solution)/shard_map/ppermute | solution.py:183
  11.1 4.5 %collective-permute-done.partner_ref = bf16[128,256]{1,0:T(8,128)(2,1)S(1)} collective-permute-done((bf16[128,256]{1,0:T(8,128)(2,1)S(1)}, bf16[128,256]{1,0:T(8,128)(2,1)S(1)}, u32[]{:S(2)}, u32[]{:S(2)}) %collective-permute-start) | collective-permute-done | bytes 65568 | tf_op jit(solution)/shard_map/ppermute | solution.py:183
  15.6 28.9 %all_gather.9.col_ref.near_ref = bf16[1024,256]{1,0:T(8,128)(2,1)S(1)} all-gather(bf16[128,256]{1,0:T(8,128)(2,1)S(1)} %collective-permute-done.partner_ref), channel_id=1, replica_groups={{0,5,8,13,16,21,24,29},{1,4,9,12,17,20,25,28},{2,7,10,15,18,23,26,31},{..., dimensions={0}, use_global_device_ids=true | all-gather | bytes 589824 | tf_op jit(solution)/shard_map/all_gather | solution.py:186
  44.5 1.9 %collective-permute-start.1 = (bf16[1024,256]{1,0:T(8,128)(2,1)S(1)}, bf16[1024,256]{1,0:T(8,128)(2,1)S(1)}, u32[]{:S(2)}, u32[]{:S(2)}) collective-permute-start(bf16[1024,256]{1,0:T(8,128)(2,1)S(1)} %all_gather.9.col_ref.near_ref), channel_id=1, source_target_pairs={{0,1},{1,0},{2,3},{3,2},{4,5},{5,4},{6,7},{7,6},{8,9},{9,8},{10,11... | collective-permute-start | bytes 1572872 | tf_op jit(solution)/shard_map/ppermute | solution.py:187
  46.5 0.0 all-to-all-done
  46.5 1.4 %shard_map.49 = (f32[4,128]{1,0:T(4,128)S(1)}, f32[8,128]{1,0:T(8,128)S(1)}) custom-call(bf16[512,256]{1,0:T(8,128)(2,1)S(1)} %bitcast.4, bf16[1024,256]{1,0:T(8,128)(2,1)S(1)} %all_gather.9.col_ref.near_ref), custom_call_target="tpu_custom_call" | custom-call | flops 536870912 | bytes 792576 | tf_op jit(solution)/shard_map/pallas_call | solution.py:155
  47.8 0.5 collective-permute-done.1.col_ref.far_ref
  48.3 1.5 %shard_map.50 = (f32[2,4,128]{2,1,0:T(4,128)S(1)}, f32[16,16,128]{2,1,0:T(8,128)}) custom-call(bf16[512,256]{1,0:T(8,128)(2,1)S(1)} %bitcast.5, bf16[1024,256]{1,0:T(8,128)(2,1)S(1)} %collective-permute-done.1.col_ref.far_ref, f32[4,128]{1,0:T(4,128)S(1)} %get-tuple-element.15.near_row_ref, f32[8,128]{1,0:T(8,128)S(1)} %get-tuple-element.16.near_col_ref), custom_call_target="tpu_custom_call" | custom-call | flops 536870912 | bytes 927744 | tf_op jit(solution)/shard_map/pallas_call | solution.py:155
  49.9 10.1 %all-to-all-start.1 = ((f32[16,16,128]{2,1,0:T(8,128)}), f32[16,16,128]{2,1,0:T(8,128)S(1)}, u32[]{:S(2)}, u32[]{:S(2)}) async-start(f32[16,16,128]{2,1,0:T(8,128)} %get-tuple-element.17), calls=%async_computation.1 | async-start | bytes 262144 | tf_op jit(solution)/shard_map/all_to_all | solution.py:174
  59.9 0.0 copy-start.1
  59.9 16.7 %all-gather = f32[8,4,128]{2,1,0:T(4,128)S(1)} all-gather(f32[2,4,128]{2,1,0:T(4,128)S(1)} %get-tuple-element.18), channel_id=2, replica_groups=mesh['pair'=2,'rest'=4,'xh'=2,'zp'=8,'z0'=2,'core'=2] {'xh','z0'}, dimensions={0}, use_global_device_ids=true | all-gather | bytes 20480 | tf_op jit(solution)/shard_map/all_gather | solution.py:203
  76.7 0.0 copy-done.1
  76.7 2.4 %shard_map.51 = (f32[4,128,256]{2,1,0:T(8,128)S(1)}, f32[1,128]{1,0:T(1,128)}, f32[1,128]{1,0:T(1,128)}, f32[128,256]{1,0:T(8,128)S(1)}) custom-call(bf16[512,256]{1,0:T(8,128)(2,1)S(1)} %bitcast.6, bf16[1024,256]{1,0:T(8,128)(2,1)S(1)} %all_gather.9.col_ref.near_ref, bf16[1024,256]{1,0:T(8,128)(2,1)S(1)} %collective-permute-done.1.col_ref.far_ref, ...), custom_call_target="tpu_custom_call" | custom-call | flops 1073741824 | bytes 2118656 | tf_op jit(solution)/shard_map/pallas_call | solution.py:155
  79.0 0.0 all-to-all-done.1.parts_ref
  79.0 0.9 shard_map.53
  79.9 3.5 %collective-permute-start.3 = (f32[128,256]{1,0:T(8,128)S(1)}, f32[128,256]{1,0:T(8,128)S(1)}, u32[]{:S(2)}, u32[]{:S(2)}) collective-permute-start(f32[128,256]{1,0:T(8,128)S(1)} %get-tuple-element.22), channel_id=1, source_target_pairs={{0,32},{32,0},{1,33},{33,1},{2,34},{34,2},{3,35},{35,3},{4,36},{36... | collective-permute-start | bytes 393224 | tf_op jit(solution)/shard_map/ppermute | solution.py:228
  83.4 5.9 %collective-permute-start.4 = (f32[128,256]{1,0:T(8,128)S(1)}, f32[128,256]{1,0:T(8,128)S(1)}, u32[]{:S(2)}, u32[]{:S(2)}) collective-permute-start(f32[128,256]{1,0:T(8,128)S(1)} %get-tuple-element.23), channel_id=1, source_target_pairs={{0,34},{2,32},{32,2},{34,0},{1,35},{3,33},{33,3},{35,1},{4,38},{6,... | collective-permute-start | bytes 393224 | tf_op jit(solution)/shard_map/ppermute | solution.py:227
  89.3 0.9 shard_map.52
  90.1 1.9 %collective-permute-start.2 = (f32[128,256]{1,0:T(8,128)S(1)}, f32[128,256]{1,0:T(8,128)S(1)}, u32[]{:S(2)}, u32[]{:S(2)}) collective-permute-start(f32[128,256]{1,0:T(8,128)S(1)} %get-tuple-element.21), channel_id=1, source_target_pairs={{0,2},{2,0},{1,3},{3,1},{4,6},{6,4},{5,7},{7,5},{8,10},{10,8},{9,1... | collective-permute-start | bytes 393224 | tf_op jit(solution)/shard_map/ppermute | solution.py:230
  92.1 0.0 collective-permute-done.3.xh_ref
  92.1 1.1 %collective-permute-done.4.both_ref = f32[128,256]{1,0:T(8,128)S(1)} collective-permute-done((f32[128,256]{1,0:T(8,128)S(1)}, f32[128,256]{1,0:T(8,128)S(1)}, u32[]{:S(2)}, u32[]{:S(2)}) %collective-permute-start.4) | collective-permute-done | bytes 131104 | tf_op jit(solution)/shard_map/ppermute | solution.py:227
  93.2 3.8 %collective-permute-done.2.z0_ref = f32[128,256]{1,0:T(8,128)S(1)} collective-permute-done((f32[128,256]{1,0:T(8,128)S(1)}, f32[128,256]{1,0:T(8,128)S(1)}, u32[]{:S(2)}, u32[]{:S(2)}) %collective-permute-start.2) | collective-permute-done | bytes 131104 | tf_op jit(solution)/shard_map/ppermute | solution.py:230
  97.0 0.7 shard_map.54
Async XLA Ops:
  2.2 5.8 %copy-start = (bf16[1,128,256]{2,1,0:T(8,128)(2,1)S(1)}, bf16[1,128,256]{2,1,0:T(8,128)(2,1)}, u32[]{:S(2)}) copy-start(bf16[1,128,256]{2,1,0:T(8,128)(2,1)} %param.2) | copy-start | bytes 196612
  2.2 44.3 %all-to-all-start = ((bf16[4,128,256]{2,1,0:T(8,128)(2,1)}), bf16[4,128,256]{2,1,0:T(8,128)(2,1)S(1)}, u32[]{:S(2)}, u32[]{:S(2)}) async-start(bf16[4,128,256]{2,1,0:T(8,128)(2,1)} %broadcast_in_dim.11), calls=%async_computation | async-start | bytes 524288 | tf_op jit(solution)/shard_map/all_to_all | solution.py:174
  8.0 7.7 %collective-permute-start = (bf16[128,256]{1,0:T(8,128)(2,1)S(1)}, bf16[128,256]{1,0:T(8,128)(2,1)S(1)}, u32[]{:S(2)}, u32[]{:S(2)}) collective-permute-start(bf16[128,256]{1,0:T(8,128)(2,1)S(1)} %bitcast.10), channel_id=1, source_target_pairs={{0,256},{256,0},{1,257},{257,1},{2,258},{258,2},{3,259},{259,3},{4... | collective-permute-start | bytes 196616 | tf_op jit(solution)/shard_map/ppermute | solution.py:183
  44.5 3.8 %collective-permute-start.1 = (bf16[1024,256]{1,0:T(8,128)(2,1)S(1)}, bf16[1024,256]{1,0:T(8,128)(2,1)S(1)}, u32[]{:S(2)}, u32[]{:S(2)}) collective-permute-start(bf16[1024,256]{1,0:T(8,128)(2,1)S(1)} %all_gather.9.col_ref.near_ref), channel_id=1, source_target_pairs={{0,1},{1,0},{2,3},{3,2},{4,5},{5,4},{6,7},{7,6},{8,9},{9,8},{10,11... | collective-permute-start | bytes 1572872 | tf_op jit(solution)/shard_map/ppermute | solution.py:187
  49.9 29.2 %all-to-all-start.1 = ((f32[16,16,128]{2,1,0:T(8,128)}), f32[16,16,128]{2,1,0:T(8,128)S(1)}, u32[]{:S(2)}, u32[]{:S(2)}) async-start(f32[16,16,128]{2,1,0:T(8,128)} %get-tuple-element.17), calls=%async_computation.1 | async-start | bytes 262144 | tf_op jit(solution)/shard_map/all_to_all | solution.py:174
  59.9 16.7 %copy-start.1 = (s32[8,128]{1,0:T(8,128)S(1)}, s32[8,128]{1,0:T(8,128)}, u32[]{:S(2)}) copy-start(s32[8,128]{1,0:T(8,128)} %positive_ref.1) | copy-start | bytes 12292
  79.9 12.2 %collective-permute-start.3 = (f32[128,256]{1,0:T(8,128)S(1)}, f32[128,256]{1,0:T(8,128)S(1)}, u32[]{:S(2)}, u32[]{:S(2)}) collective-permute-start(f32[128,256]{1,0:T(8,128)S(1)} %get-tuple-element.22), channel_id=1, source_target_pairs={{0,32},{32,0},{1,33},{33,1},{2,34},{34,2},{3,35},{35,3},{4,36},{36... | collective-permute-start | bytes 393224 | tf_op jit(solution)/shard_map/ppermute | solution.py:228
  83.4 9.8 %collective-permute-start.4 = (f32[128,256]{1,0:T(8,128)S(1)}, f32[128,256]{1,0:T(8,128)S(1)}, u32[]{:S(2)}, u32[]{:S(2)}) collective-permute-start(f32[128,256]{1,0:T(8,128)S(1)} %get-tuple-element.23), channel_id=1, source_target_pairs={{0,34},{2,32},{32,2},{34,0},{1,35},{3,33},{33,3},{35,1},{4,38},{6,... | collective-permute-start | bytes 393224 | tf_op jit(solution)/shard_map/ppermute | solution.py:227
  90.1 6.9 %collective-permute-start.2 = (f32[128,256]{1,0:T(8,128)S(1)}, f32[128,256]{1,0:T(8,128)S(1)}, u32[]{:S(2)}, u32[]{:S(2)}) collective-permute-start(f32[128,256]{1,0:T(8,128)S(1)} %get-tuple-element.21), channel_id=1, source_target_pairs={{0,2},{2,0},{1,3},{3,1},{4,6},{6,4},{5,7},{7,5},{8,10},{10,8},{9,1... | collective-permute-start | bytes 393224 | tf_op jit(solution)/shard_map/ppermute | solution.py:230
